TPU v7x, 32 devices: a whole 2x2x4 slice. The times are simulated.
32 devices in a mesh: parts: 2 (over y), blk: 8 (over z, x), sub: 2 (over core).
Axes of the slice: x: 2, y: 2, z: 4, core: 2. Of those that a mesh axis runs over, the one named last changes fastest.
Arguments:
- embeddings: bfloat16 [24576, 1024], P(('parts', 'blk', 'sub')), parts along dimension 0, may hold values from -6 to 6
- labels: int32 [24576], P(('parts', 'blk', 'sub')), parts along dimension 0, may hold values from 0 to 127, as said below
Outputs:
- dedup_weight: float32 [24576], P(('parts', 'blk', 'sub')), parts along dimension 0
- cluster_mass: float32 [256], P('parts'), parts along dimension 0
There are 2 independent parts, one for each index of `parts`. A program takes and returns all parts, laid end to end along the dimension named above; each array names one. Nothing has to cross between parts.
Inputs may be any that keep to these rules, and one draw needn't show every extreme that they name: `labels`: every label of 0 to 127 occurs.
All inputs are finite; a program needn't handle non-finite values.
Results may differ from a plain program's by a relative error of at most 0.0003.
Values may be sent and summed in bfloat16 or wider, within the bound.
No kernel may reach another device: no remote copies, remote signals or barrier semaphores. Data moves between devices by JAX's collectives and lax.ppermute only.
A program may use at most 64 MiB of HBM per device.

v0:
```python
import functools
import math

import jax
import jax.numpy as jnp
from jax import lax
from jax.experimental import pallas as pl
from jax.experimental.pallas import tpu as pltpu
from jax.sharding import PartitionSpec as P

CLUSTERS = 128
TAU = 25.0
LOG2E = math.log2(math.e)
AXES = ("blk", "sub")
LANES = 128
VMEM = pl.BlockSpec(memory_space=pltpu.VMEM)
SMEM = pl.BlockSpec(memory_space=pltpu.SMEM)
PARAMS = pltpu.CompilerParams(vmem_limit_bytes=16 << 20)


def exchange(value, xor):
    count = lax.axis_size("blk") * lax.axis_size("sub")
    return lax.ppermute(value, AXES, [(i, i ^ xor) for i in range(count)])


def exchange_flipped(value, chip_bit, flip):
    pairs = []
    for blk in range(lax.axis_size("blk")):
        for sub in range(2):
            source = (blk ^ (1 << chip_bit)) * 2 + (sub ^ flip(blk))
            pairs.append((source, blk * 2 + sub))
    return lax.ppermute(value, AXES, pairs)


def flip_x(blk):
    return (blk ^ (blk >> 1)) & 1


def flip_z(blk):
    return (blk >> 1) & 1


def down_rows(lab, first, size):
    pieces = []
    for at in range(first, first + size, LANES):
        n = min(LANES, first + size - at)
        pieces.append(jnp.broadcast_to(lab[:, at : at + n], (LANES, n)).T)
    return pieces[0] if len(pieces) == 1 else jnp.concatenate(pieces, axis=0)


def tile(rows, down, cols_ref, lab_ref, sum_ref, start, size, width, step, fold=True):
    m = rows.shape[0]
    scale = TAU * LOG2E / width
    folded = jnp.zeros((m, LANES), jnp.float32)
    for at in range(0, size, step):
        n = min(step, size - at)
        score = lax.dot_general(
            rows, cols_ref[at : at + n, :], (((1,), (1,)), ((), ())), preferred_element_type=jnp.float32
        )
        power = jnp.exp2(score * scale - TAU * LOG2E)
        for lane in range(0, n, LANES):
            there = slice(start + at + lane, start + at + lane + LANES)
            value = jnp.where(down == lab_ref[:, there], power[:, lane : lane + LANES], 0.0)
            sum_ref[:, there] += jnp.sum(value, axis=0, keepdims=True)
            if fold:
                folded = folded + value
    return folded


def to_lanes(folded):
    return jnp.sum(folded.T, axis=0, keepdims=True)


def near_kernel(own_ref, other_ref, own_row, other_row, out_ref, *, width):
    out_ref[...] = jnp.zeros_like(out_ref)
    count = own_ref.shape[0]
    for rows_ref, lab in ((own_ref, own_row), (other_ref, other_row)):
        for at in range(0, count, 256):
            m = min(256, count - at)
            tile(rows_ref[at : at + m, :], down_rows(lab, at, m), own_ref, own_row, out_ref, 0, count, width, 256, False)


def near(own, other, own_row, other_row):
    count, width = own.shape
    return pl.pallas_call(
        functools.partial(near_kernel, width=width),
        out_shape=jax.ShapeDtypeStruct((1, count), jnp.float32),
        in_specs=[VMEM] * 4,
        out_specs=VMEM,
        compiler_params=PARAMS,
        cost_estimate=pl.CostEstimate(
            flops=4 * count * count * width, bytes_accessed=4 * count * width, transcendentals=2 * count * count
        ),
    )(own, other, own_row, other_row)


def far_kernel(*refs, count, width, chunks, last):
    k = len(chunks) - 1
    xs, zs = refs[: k + 1], refs[k + 1 : 2 * k + 2]
    own, own_row, x_row, z_row, own_in, x_in, z_in, turns = refs[2 * k + 2 : 2 * k + 10]
    outs = refs[2 * k + 10 :]
    own_sum, x_sum, z_sum = outs[-3:]
    own_sum[...] = own_in[...]
    x_sum[...] = x_in[...]
    z_sum[...] = z_in[...]
    size = chunks[k]
    first = sum(chunks[:k])
    x_new, z_new = xs[k][...], zs[k][...]
    down_x, down_z = down_rows(x_row, first, size), down_rows(z_row, first, size)
    fold_x = tile(x_new, down_x, own, own_row, own_sum, 0, count, width, 256)
    fold_z = tile(z_new, down_z, own, own_row, own_sum, 0, count, width, 256)
    at = 0
    for j in range(k + 1):
        n = chunks[j]
        fold_x = fold_x + tile(x_new, down_x, zs[j], z_row, z_sum, at, n, width, 256)
        if j < k:
            fold_z = fold_z + tile(z_new, down_z, xs[j], x_row, x_sum, at, n, width, 256)
        at += n
    x_sum[:, first : first + size] += to_lanes(fold_x)
    z_sum[:, first : first + size] += to_lanes(fold_z)
    if last:
        part = outs[0]
        zero = jnp.zeros((1, count), jnp.float32)
        turn_x, turn_z = turns[0] == 1, turns[1] == 1
        part[0:1, :] = own_sum[...]
        part[1:2, :] = zero
        part[2:3, :] = jnp.where(turn_x, zero, x_sum[...])
        part[3:4, :] = jnp.where(turn_x, x_sum[...], zero)
        part[4:5, :] = jnp.where(turn_z, zero, z_sum[...])
        part[5:6, :] = jnp.where(turn_z, z_sum[...], zero)
        part[6:7, :] = zero
        part[7:8, :] = zero


def far(xs, zs, own, own_row, x_row, z_row, sums, turns, chunks):
    count, width = own.shape
    k = len(xs) - 1
    last = k == len(chunks) - 1
    pairs = 2 * chunks[k] * count + chunks[k] * (2 * sum(chunks[:k]) + chunks[k])
    row = jax.ShapeDtypeStruct((1, count), jnp.float32)
    return pl.pallas_call(
        functools.partial(far_kernel, count=count, width=width, chunks=tuple(chunks[: k + 1]), last=last),
        out_shape=jax.ShapeDtypeStruct((8, count), jnp.float32) if last else [row] * 3,
        in_specs=[VMEM] * (2 * k + 9) + [SMEM],
        out_specs=VMEM if last else [VMEM] * 3,
        scratch_shapes=[pltpu.VMEM((1, count), jnp.float32)] * 3 if last else [],
        compiler_params=PARAMS,
        cost_estimate=pl.CostEstimate(
            flops=2 * pairs * width, bytes_accessed=2 * width * (count + 2 * sum(chunks[: k + 1])), transcendentals=pairs
        ),
    )(*xs, *zs, own, own_row, x_row, z_row, *sums, turns)


def cut(count):
    if count % 256 == 0 and count > 256:
        return [256] * (count // 256 - 1) + [128, 128]
    if count % 128 == 0:
        return [128] * (count // 128)
    return [count]


def per_device(embeddings, labels):
    count, _ = embeddings.shape
    blk = lax.axis_index("blk")
    chunks = cut(count)
    turns = jnp.stack([flip_x(blk), flip_z(blk)]).astype(jnp.int32)
    lab = labels[None, :]
    xs, zs = [], []

    def send(source, at, n):
        piece = lax.slice_in_dim(source, at, at + n, axis=0)
        xs.append(exchange_flipped(piece, 0, flip_x))
        zs.append(exchange_flipped(piece, 1, flip_z))

    send(embeddings, 0, chunks[0])
    other = exchange(lab, 1)
    lab_s = jnp.concatenate([lab, other], axis=0)
    lab_x = exchange(lab_s, 2)
    lab_z = exchange(lab_s, 4)
    source, lab_s, lab = lax.optimization_barrier((embeddings, lab_s, lab))
    at = chunks[0]
    for k, n in enumerate(chunks[1:], 1):
        send(source, at, n)
        at += n
    lab_d = exchange(lab_x, 4)
    partner = exchange(source, 1)
    lab_all = jnp.concatenate([lab_s, lab_x, lab_z, lab_d], axis=0)
    x_lab = jnp.where(turns[0] == 1, lab_x[1:2], lab_x[0:1])
    z_lab = jnp.where(turns[1] == 1, lab_z[1:2], lab_z[0:1])

    own_sum = near(embeddings, partner, lab, other)
    zero = jnp.zeros((1, count), jnp.float32)
    sums = (own_sum, zero, zero)
    for k in range(len(chunks)):
        sums = far(xs[: k + 1], zs[: k + 1], embeddings, lab, x_lab, z_lab, sums, turns, chunks)
    part = sums

    def turned(a, bit):
        return jnp.concatenate([a[r ^ bit : (r ^ bit) + 1] for r in range(8)], axis=0)

    for bit in (1, 2, 4):
        part = part + turned(exchange(part, bit), bit)
    weight = 1.0 / part
    ident = jnp.arange(CLUSTERS, dtype=jnp.int32)
    mass = jnp.sum(jnp.where(lab_all[:, None, :] == ident[None, :, None], weight[:, None, :], 0.0), axis=(0, 2))
    bit = 8
    while bit < lax.axis_size("blk") * 2:
        mass = mass + exchange(mass, bit)
        bit *= 2
    return weight[0], mass


def solution(mesh):
    in_specs = (P(("parts", "blk", "sub"), None), P(("parts", "blk", "sub")))
    out_specs = (P(("parts", "blk", "sub")), P("parts"))
    return jax.shard_map(per_device, mesh=mesh, in_specs=in_specs, out_specs=out_specs, check_vma=False)
```

profile of v0, /device:TPU:0, one launch (start us, length us, event | category | flops | bytes accessed | tf_op | source)
XLA Modules:
  0.0 63.9 jit_solution(14139899588763328591)
XLA Ops:
  0.6 0.8 %broadcast_in_dim.21.own_row.refs_3_.refs_5_.refs_7_.refs_9_ = s32[1,768]{1,0:T(1,128)S(1)} reshape(s32[768]{0:T(1024)} %param.3) | data formatting | bytes 6144 | tf_op jit(solution)/shard_map/broadcast_in_dim | solution.py:167
  1.4 0.5 collective-permute-start.1
  1.9 0.8 %collective-permute-done.1.other_row = s32[1,768]{1,0:T(1,128)S(1)} collective-permute-done((s32[1,768]{1,0:T(1,128)S(1)}, s32[1,768]{1,0:T(1,128)S(1)}, u32[]{:S(2)}, u32[]{:S(2)}) %collective-permute-start.1) | collective-permute-done | bytes 3104 | tf_op jit(solution)/shard_map/ppermute | solution.py:23
  3.2 1.1 %slice.85 = bf16[256,1024]{1,0:T(8,128)(2,1)S(1)} slice(bf16[768,1024]{1,0:T(8,128)(2,1)} %refs_8_.1), slice={[0:256], [0:1024]} | slice | bytes 1048576 | tf_op jit(solution)/shard_map/slice | solution.py:171
  4.3 2.6 %collective-permute-start = (bf16[256,1024]{1,0:T(8,128)(2,1)S(1)}, bf16[256,1024]{1,0:T(8,128)(2,1)S(1)}, u32[]{:S(2)}, u32[]{:S(2)}) collective-permute-start(bf16[256,1024]{1,0:T(8,128)(2,1)S(1)} %slice.85), channel_id=1, source_target_pairs={{2,0},{3,1},{1,2},{0,3},{7,4},{6,5},{4,6},{5,7},{10,8},{11,9},{9,1... | collective-permute-start | bytes 1572872 | tf_op jit(solution)/shard_map/ppermute | solution.py:32
  6.9 1.3 %collective-permute-start.5 = (bf16[256,1024]{1,0:T(8,128)(2,1)S(1)}, bf16[256,1024]{1,0:T(8,128)(2,1)S(1)}, u32[]{:S(2)}, u32[]{:S(2)}) collective-permute-start(bf16[256,1024]{1,0:T(8,128)(2,1)S(1)} %slice.85), channel_id=1, source_target_pairs={{4,0},{5,1},{6,2},{7,3},{1,4},{0,5},{3,6},{2,7},{12,8},{13,9},{14,... | collective-permute-start | bytes 1572872 | tf_op jit(solution)/shard_map/ppermute | solution.py:32
  8.3 0.6 collective-permute-start.9
  9.1 1.1 %fusion.1 = (bf16[128,1024]{1,0:T(8,128)(2,1)S(1)}, bf16[128,1024]{1,0:T(8,128)(2,1)S(1)}) fusion(bf16[768,1024]{1,0:T(8,128)(2,1)} %refs_8_.1), kind=kLoop, calls=%fused_computation.11 | loop fusion | bytes 1048576 | tf_op jit(solution)/shard_map/slice | solution.py:171
  10.2 9.3 %collective-permute-done.9 = s32[2,768]{1,0:T(2,128)S(1)} collective-permute-done((s32[2,768]{1,0:T(2,128)S(1)}, s32[2,768]{1,0:T(2,128)S(1)}, u32[]{:S(2)}, u32[]{:S(2)}) %collective-permute-start.9) | collective-permute-done | bytes 6176 | tf_op jit(solution)/shard_map/ppermute | solution.py:23
  19.5 1.0 %collective-permute-start.2 = (bf16[256,1024]{1,0:T(8,128)(2,1)S(1)}, bf16[256,1024]{1,0:T(8,128)(2,1)S(1)}, u32[]{:S(2)}, u32[]{:S(2)}) collective-permute-start(bf16[256,1024]{1,0:T(8,128)(2,1)S(1)} %slice.86), channel_id=1, source_target_pairs={{2,0},{3,1},{1,2},{0,3},{7,4},{6,5},{4,6},{5,7},{10,8},{11,9},{9,1... | collective-permute-start | bytes 1572872 | tf_op jit(solution)/shard_map/ppermute | solution.py:32
  20.5 0.5 collective-permute-done.10
  21.0 1.2 %collective-permute-start.6 = (bf16[256,1024]{1,0:T(8,128)(2,1)S(1)}, bf16[256,1024]{1,0:T(8,128)(2,1)S(1)}, u32[]{:S(2)}, u32[]{:S(2)}) collective-permute-start(bf16[256,1024]{1,0:T(8,128)(2,1)S(1)} %slice.86), channel_id=1, source_target_pairs={{4,0},{5,1},{6,2},{7,3},{1,4},{0,5},{3,6},{2,7},{12,8},{13,9},{14,... | collective-permute-start | bytes 1572872 | tf_op jit(solution)/shard_map/ppermute | solution.py:32
  22.2 0.9 %collective-permute-start.3 = (bf16[128,1024]{1,0:T(8,128)(2,1)S(1)}, bf16[128,1024]{1,0:T(8,128)(2,1)S(1)}, u32[]{:S(2)}, u32[]{:S(2)}) collective-permute-start(bf16[128,1024]{1,0:T(8,128)(2,1)S(1)} %get-tuple-element.27), channel_id=1, source_target_pairs={{2,0},{3,1},{1,2},{0,3},{7,4},{6,5},{4,6},{5,7},{10,8},{11,9},{9,1... | collective-permute-start | bytes 786440 | tf_op jit(solution)/shard_map/ppermute | solution.py:32
  23.2 4.6 %shard_map.41.refs_6_ = f32[1,768]{1,0:T(1,128)S(1)} custom-call(bf16[768,1024]{1,0:T(8,128)(2,1)S(1)} %copy-done, bf16[768,1024]{1,0:T(8,128)(2,1)} %collective-permute-done.11.other_ref, s32[1,768]{1,0:T(1,128)S(1)} %broadcast_in_dim.21.own_row.refs_3_.refs_5_.refs_7_.refs_9_, s32[1,768]{1,0:T(1,128)S(1)} %collective-permute-done.1.other_row), custom_call_target="tpu_custom_call" | custom-call | flops 2415919104 | bytes 3145728 | tf_op jit(solution)/shard_map/pallas_call | solution.py:85
  27.8 1.5 %collective-permute-start.4 = (bf16[128,1024]{1,0:T(8,128)(2,1)S(1)}, bf16[128,1024]{1,0:T(8,128)(2,1)S(1)}, u32[]{:S(2)}, u32[]{:S(2)}) collective-permute-start(bf16[128,1024]{1,0:T(8,128)(2,1)S(1)} %get-tuple-element.26), channel_id=1, source_target_pairs={{2,0},{3,1},{1,2},{0,3},{7,4},{6,5},{4,6},{5,7},{10,8},{11,9},{9,1... | collective-permute-start | bytes 786440 | tf_op jit(solution)/shard_map/ppermute | solution.py:32
  29.3 5.0 %collective-permute-done.2.refs_1_ = bf16[256,1024]{1,0:T(8,128)(2,1)S(1)} collective-permute-done((bf16[256,1024]{1,0:T(8,128)(2,1)S(1)}, bf16[256,1024]{1,0:T(8,128)(2,1)S(1)}, u32[]{:S(2)}, u32[]{:S(2)}) %collective-permute-start.2) | collective-permute-done | bytes 524320 | tf_op jit(solution)/shard_map/ppermute | solution.py:32
  34.3 1.0 %collective-permute-start.8 = (bf16[128,1024]{1,0:T(8,128)(2,1)S(1)}, bf16[128,1024]{1,0:T(8,128)(2,1)S(1)}, u32[]{:S(2)}, u32[]{:S(2)}) collective-permute-start(bf16[128,1024]{1,0:T(8,128)(2,1)S(1)} %get-tuple-element.26), channel_id=1, source_target_pairs={{4,0},{5,1},{6,2},{7,3},{1,4},{0,5},{3,6},{2,7},{12,8},{13,9},{14,... | collective-permute-start | bytes 786440 | tf_op jit(solution)/shard_map/ppermute | solution.py:32
  35.3 1.9 %shard_map.42 = (f32[1,768]{1,0:T(1,128)S(1)}, f32[1,768]{1,0:T(1,128)S(1)}, f32[1,768]{1,0:T(1,128)S(1)}) custom-call(bf16[256,1024]{1,0:T(8,128)(2,1)S(1)} %collective-permute-done.refs_0_, bf16[256,1024]{1,0:T(8,128)(2,1)S(1)} %collective-permute-done.5.refs_1_.refs_2_.refs_3_.refs_4_, bf16[768,1024]{1,0:T(8,128)(2,1)S(1)} %copy-done, ...), custom_call_target="tpu_custom_call" | custom-call | flops 939524096 | bytes 2621440 | tf_op jit(solution)/shard_map/pallas_call | solution.py:141
  37.2 2.2 %shard_map.43 = (f32[1,768]{1,0:T(1,128)S(1)}, f32[1,768]{1,0:T(1,128)S(1)}, f32[1,768]{1,0:T(1,128)S(1)}) custom-call(bf16[256,1024]{1,0:T(8,128)(2,1)S(1)} %collective-permute-done.refs_0_, bf16[256,1024]{1,0:T(8,128)(2,1)S(1)} %collective-permute-done.2.refs_1_, bf16[256,1024]{1,0:T(8,128)(2,1)S(1)} %collective-permute-done.5.refs_1_.refs_2_.refs_3_.refs_4_, ...), custom_call_target="tpu_custom_call" | custom-call | flops 1207959552 | bytes 3670016 | tf_op jit(solution)/shard_map/pallas_call | solution.py:141
  39.9 1.5 %collective-permute-done.7.refs_5_.refs_6_ = bf16[128,1024]{1,0:T(8,128)(2,1)S(1)} collective-permute-done((bf16[128,1024]{1,0:T(8,128)(2,1)S(1)}, bf16[128,1024]{1,0:T(8,128)(2,1)S(1)}, u32[]{:S(2)}, u32[]{:S(2)}) %collective-permute-start.7) | collective-permute-done | bytes 262176 | tf_op jit(solution)/shard_map/ppermute | solution.py:32
  41.4 2.5 %shard_map.44 = (f32[1,768]{1,0:T(1,128)S(1)}, f32[1,768]{1,0:T(1,128)S(1)}, f32[1,768]{1,0:T(1,128)S(1)}) custom-call(bf16[256,1024]{1,0:T(8,128)(2,1)S(1)} %collective-permute-done.refs_0_, bf16[256,1024]{1,0:T(8,128)(2,1)S(1)} %collective-permute-done.2.refs_1_, bf16[128,1024]{1,0:T(8,128)(2,1)S(1)} %collective-permute-done.3.refs_2_, ...), custom_call_target="tpu_custom_call" | custom-call | flops 704643072 | bytes 4194304 | tf_op jit(solution)/shard_map/pallas_call | solution.py:141
  44.4 2.2 %collective-permute-done.8.refs_7_ = bf16[128,1024]{1,0:T(8,128)(2,1)S(1)} collective-permute-done((bf16[128,1024]{1,0:T(8,128)(2,1)S(1)}, bf16[128,1024]{1,0:T(8,128)(2,1)S(1)}, u32[]{:S(2)}, u32[]{:S(2)}) %collective-permute-start.8) | collective-permute-done | bytes 262176 | tf_op jit(solution)/shard_map/ppermute | solution.py:32
  46.6 2.7 %shard_map.45 = f32[8,768]{1,0:T(8,128)S(1)} custom-call(bf16[256,1024]{1,0:T(8,128)(2,1)S(1)} %collective-permute-done.refs_0_, bf16[256,1024]{1,0:T(8,128)(2,1)S(1)} %collective-permute-done.2.refs_1_, bf16[128,1024]{1,0:T(8,128)(2,1)S(1)} %collective-permute-done.3.refs_2_, bf16[128,1024]{1,0:T(8,128)(2,1)S(1)} %collective-permute-done.4.refs_3_, ...), custom_call_target="tpu_custom_call" | custom-call | flops 771751936 | bytes 4718592 | tf_op jit(solution)/shard_map/pallas_call | solution.py:141
  49.3 1.2 %collective-permute-done.12 = f32[8,768]{1,0:T(8,128)S(1)} collective-permute-done((f32[8,768]{1,0:T(8,128)S(1)}, f32[8,768]{1,0:T(8,128)S(1)}, u32[]{:S(2)}, u32[]{:S(2)}) %collective-permute-start.12) | collective-permute-done | bytes 24608 | tf_op jit(solution)/shard_map/ppermute | solution.py:23
  51.0 1.5 %collective-permute-start.15 = (s32[2,768]{1,0:T(2,128)S(1)}, s32[2,768]{1,0:T(2,128)S(1)}, u32[]{:S(2)}, u32[]{:S(2)}) collective-permute-start(s32[2,768]{1,0:T(2,128)S(1)} %collective-permute-done.9), channel_id=1, source_target_pairs={{0,4},{1,5},{2,6},{3,7},{4,0},{5,1},{6,2},{7,3},{8,12},{9,13},{10,... | collective-permute-start | bytes 18440 | tf_op jit(solution)/shard_map/ppermute | solution.py:23
  52.5 2.0 %collective-permute-done.13 = f32[8,768]{1,0:T(8,128)S(1)} collective-permute-done((f32[8,768]{1,0:T(8,128)S(1)}, f32[8,768]{1,0:T(8,128)S(1)}, u32[]{:S(2)}, u32[]{:S(2)}) %collective-permute-start.13) | collective-permute-done | bytes 24608 | tf_op jit(solution)/shard_map/ppermute | solution.py:23
  54.5 1.8 %collective-permute-start.14 = (f32[8,768]{1,0:T(8,128)S(1)}, f32[8,768]{1,0:T(8,128)S(1)}, u32[]{:S(2)}, u32[]{:S(2)}) collective-permute-start(f32[8,768]{1,0:T(8,128)S(1)} %maximum_add_fusion), channel_id=1, source_target_pairs={{0,4},{1,5},{2,6},{3,7},{4,0},{5,1},{6,2},{7,3},{8,12},{9,13},{10,... | collective-permute-start | bytes 73736 | tf_op jit(solution)/shard_map/ppermute | solution.py:23
  56.3 2.1 %collective-permute-done.14 = f32[8,768]{1,0:T(8,128)S(1)} collective-permute-done((f32[8,768]{1,0:T(8,128)S(1)}, f32[8,768]{1,0:T(8,128)S(1)}, u32[]{:S(2)}, u32[]{:S(2)}) %collective-permute-start.14) | collective-permute-done | bytes 24608 | tf_op jit(solution)/shard_map/ppermute | solution.py:23
  58.8 2.6 %collective-permute-start.16 = (f32[128]{0:T(128)S(1)}, f32[128]{0:T(128)S(1)}, u32[]{:S(2)}, u32[]{:S(2)}) collective-permute-start(f32[128]{0:T(128)S(1)} %select_reduce_fusion), channel_id=1, source_target_pairs={{0,8},{1,9},{2,10},{3,11},{4,12},{5,13},{6,14},{7,15},{8,0},{9,1},... | collective-permute-start | bytes 1544 | tf_op jit(solution)/shard_map/ppermute | solution.py:23
  61.5 0.6 slice_reduce_fusion
  62.1 1.3 %collective-permute-done.16 = f32[128]{0:T(128)S(1)} collective-permute-done((f32[128]{0:T(128)S(1)}, f32[128]{0:T(128)S(1)}, u32[]{:S(2)}, u32[]{:S(2)}) %collective-permute-start.16) | collective-permute-done | bytes 544 | tf_op jit(solution)/shard_map/ppermute | solution.py:23
  63.3 0.5 add.15
  (29 shorter events, 2.7 us)
Async XLA Ops:
  0.6 9.6 %copy-start = (bf16[768,1024]{1,0:T(8,128)(2,1)S(1)}, bf16[768,1024]{1,0:T(8,128)(2,1)}, u32[]{:S(2)}) copy-start(bf16[768,1024]{1,0:T(8,128)(2,1)} %refs_8_.1) | copy-start | bytes 4718596
  1.4 1.3 %collective-permute-start.1 = (s32[1,768]{1,0:T(1,128)S(1)}, s32[1,768]{1,0:T(1,128)S(1)}, u32[]{:S(2)}, u32[]{:S(2)}) collective-permute-start(s32[1,768]{1,0:T(1,128)S(1)} %broadcast_in_dim.21.own_row.refs_3_.refs_5_.refs_7_.refs_9_), channel_id=1, source_target_pairs={{0,1},{1,0},{2,3},{3,2},{4,5},{5,4},{6,7},{7,6},{8,9},{9,8},{10,11... | collective-permute-start | bytes 9224 | tf_op jit(solution)/shard_map/ppermute | solution.py:23
  2.8 20.4 %collective-permute-start.11 = (bf16[768,1024]{1,0:T(8,128)(2,1)}, bf16[768,1024]{1,0:T(8,128)(2,1)}, u32[]{:S(2)}, u32[]{:S(2)}) collective-permute-start(bf16[768,1024]{1,0:T(8,128)(2,1)} %refs_8_.1), channel_id=1, source_target_pairs={{0,1},{1,0},{2,3},{3,2},{4,5},{5,4},{6,7},{7,6},{8,9},{9,8},{10,11... | collective-permute-start | bytes 4718600 | tf_op jit(solution)/shard_map/ppermute | solution.py:23
  4.3 18.0 %collective-permute-start = (bf16[256,1024]{1,0:T(8,128)(2,1)S(1)}, bf16[256,1024]{1,0:T(8,128)(2,1)S(1)}, u32[]{:S(2)}, u32[]{:S(2)}) collective-permute-start(bf16[256,1024]{1,0:T(8,128)(2,1)S(1)} %slice.85), channel_id=1, source_target_pairs={{2,0},{3,1},{1,2},{0,3},{7,4},{6,5},{4,6},{5,7},{10,8},{11,9},{9,1... | collective-permute-start | bytes 1572872 | tf_op jit(solution)/shard_map/ppermute | solution.py:32
  6.9 20.9 %collective-permute-start.5 = (bf16[256,1024]{1,0:T(8,128)(2,1)S(1)}, bf16[256,1024]{1,0:T(8,128)(2,1)S(1)}, u32[]{:S(2)}, u32[]{:S(2)}) collective-permute-start(bf16[256,1024]{1,0:T(8,128)(2,1)S(1)} %slice.85), channel_id=1, source_target_pairs={{4,0},{5,1},{6,2},{7,3},{1,4},{0,5},{3,6},{2,7},{12,8},{13,9},{14,... | collective-permute-start | bytes 1572872 | tf_op jit(solution)/shard_map/ppermute | solution.py:32
  8.3 11.2 %collective-permute-start.9 = (s32[2,768]{1,0:T(2,128)S(1)}, s32[2,768]{1,0:T(2,128)S(1)}, u32[]{:S(2)}, u32[]{:S(2)}) collective-permute-start(s32[2,768]{1,0:T(2,128)S(1)} %pad_add_fusion.1), channel_id=1, source_target_pairs={{0,2},{1,3},{2,0},{3,1},{4,6},{5,7},{6,4},{7,5},{8,10},{9,11},{10,... | collective-permute-start | bytes 18440 | tf_op jit(solution)/shard_map/ppermute | solution.py:23
  8.9 12.2 %collective-permute-start.10 = (s32[2,768]{1,0:T(2,128)S(1)}, s32[2,768]{1,0:T(2,128)S(1)}, u32[]{:S(2)}, u32[]{:S(2)}) collective-permute-start(s32[2,768]{1,0:T(2,128)S(1)} %pad_add_fusion.1), channel_id=1, source_target_pairs={{0,4},{1,5},{2,6},{3,7},{4,0},{5,1},{6,2},{7,3},{8,12},{9,13},{10,... | collective-permute-start | bytes 18440 | tf_op jit(solution)/shard_map/ppermute | solution.py:23
  19.5 14.8 %collective-permute-start.2 = (bf16[256,1024]{1,0:T(8,128)(2,1)S(1)}, bf16[256,1024]{1,0:T(8,128)(2,1)S(1)}, u32[]{:S(2)}, u32[]{:S(2)}) collective-permute-start(bf16[256,1024]{1,0:T(8,128)(2,1)S(1)} %slice.86), channel_id=1, source_target_pairs={{2,0},{3,1},{1,2},{0,3},{7,4},{6,5},{4,6},{5,7},{10,8},{11,9},{9,1... | collective-permute-start | bytes 1572872 | tf_op jit(solution)/shard_map/ppermute | solution.py:32
  21.0 16.2 %collective-permute-start.6 = (bf16[256,1024]{1,0:T(8,128)(2,1)S(1)}, bf16[256,1024]{1,0:T(8,128)(2,1)S(1)}, u32[]{:S(2)}, u32[]{:S(2)}) collective-permute-start(bf16[256,1024]{1,0:T(8,128)(2,1)S(1)} %slice.86), channel_id=1, source_target_pairs={{4,0},{5,1},{6,2},{7,3},{1,4},{0,5},{3,6},{2,7},{12,8},{13,9},{14,... | collective-permute-start | bytes 1572872 | tf_op jit(solution)/shard_map/ppermute | solution.py:32
  22.2 17.7 %collective-permute-start.3 = (bf16[128,1024]{1,0:T(8,128)(2,1)S(1)}, bf16[128,1024]{1,0:T(8,128)(2,1)S(1)}, u32[]{:S(2)}, u32[]{:S(2)}) collective-permute-start(bf16[128,1024]{1,0:T(8,128)(2,1)S(1)} %get-tuple-element.27), channel_id=1, source_target_pairs={{2,0},{3,1},{1,2},{0,3},{7,4},{6,5},{4,6},{5,7},{10,8},{11,9},{9,1... | collective-permute-start | bytes 786440 | tf_op jit(solution)/shard_map/ppermute | solution.py:32
  23.2 18.3 %collective-permute-start.7 = (bf16[128,1024]{1,0:T(8,128)(2,1)S(1)}, bf16[128,1024]{1,0:T(8,128)(2,1)S(1)}, u32[]{:S(2)}, u32[]{:S(2)}) collective-permute-start(bf16[128,1024]{1,0:T(8,128)(2,1)S(1)} %get-tuple-element.27), channel_id=1, source_target_pairs={{4,0},{5,1},{6,2},{7,3},{1,4},{0,5},{3,6},{2,7},{12,8},{13,9},{14,... | collective-permute-start | bytes 786440 | tf_op jit(solution)/shard_map/ppermute | solution.py:32
  27.8 16.6 %collective-permute-start.4 = (bf16[128,1024]{1,0:T(8,128)(2,1)S(1)}, bf16[128,1024]{1,0:T(8,128)(2,1)S(1)}, u32[]{:S(2)}, u32[]{:S(2)}) collective-permute-start(bf16[128,1024]{1,0:T(8,128)(2,1)S(1)} %get-tuple-element.26), channel_id=1, source_target_pairs={{2,0},{3,1},{1,2},{0,3},{7,4},{6,5},{4,6},{5,7},{10,8},{11,9},{9,1... | collective-permute-start | bytes 786440 | tf_op jit(solution)/shard_map/ppermute | solution.py:32
  34.3 12.2 %collective-permute-start.8 = (bf16[128,1024]{1,0:T(8,128)(2,1)S(1)}, bf16[128,1024]{1,0:T(8,128)(2,1)S(1)}, u32[]{:S(2)}, u32[]{:S(2)}) collective-permute-start(bf16[128,1024]{1,0:T(8,128)(2,1)S(1)} %get-tuple-element.26), channel_id=1, source_target_pairs={{4,0},{5,1},{6,2},{7,3},{1,4},{0,5},{3,6},{2,7},{12,8},{13,9},{14,... | collective-permute-start | bytes 786440 | tf_op jit(solution)/shard_map/ppermute | solution.py:32
  49.2 1.3 %collective-permute-start.12 = (f32[8,768]{1,0:T(8,128)S(1)}, f32[8,768]{1,0:T(8,128)S(1)}, u32[]{:S(2)}, u32[]{:S(2)}) collective-permute-start(f32[8,768]{1,0:T(8,128)S(1)} %shard_map.45), channel_id=1, source_target_pairs={{0,1},{1,0},{2,3},{3,2},{4,5},{5,4},{6,7},{7,6},{8,9},{9,8},{10,11... | collective-permute-start | bytes 73736 | tf_op jit(solution)/shard_map/ppermute | solution.py:23
  50.6 3.9 %collective-permute-start.13 = (f32[8,768]{1,0:T(8,128)S(1)}, f32[8,768]{1,0:T(8,128)S(1)}, u32[]{:S(2)}, u32[]{:S(2)}) collective-permute-start(f32[8,768]{1,0:T(8,128)S(1)} %add.12), channel_id=1, source_target_pairs={{0,2},{1,3},{2,0},{3,1},{4,6},{5,7},{6,4},{7,5},{8,10},{9,11},{10,... | collective-permute-start | bytes 73736 | tf_op jit(solution)/shard_map/ppermute | solution.py:23
  51.0 5.3 %collective-permute-start.15 = (s32[2,768]{1,0:T(2,128)S(1)}, s32[2,768]{1,0:T(2,128)S(1)}, u32[]{:S(2)}, u32[]{:S(2)}) collective-permute-start(s32[2,768]{1,0:T(2,128)S(1)} %collective-permute-done.9), channel_id=1, source_target_pairs={{0,4},{1,5},{2,6},{3,7},{4,0},{5,1},{6,2},{7,3},{8,12},{9,13},{10,... | collective-permute-start | bytes 18440 | tf_op jit(solution)/shard_map/ppermute | solution.py:23
  54.5 3.9 %collective-permute-start.14 = (f32[8,768]{1,0:T(8,128)S(1)}, f32[8,768]{1,0:T(8,128)S(1)}, u32[]{:S(2)}, u32[]{:S(2)}) collective-permute-start(f32[8,768]{1,0:T(8,128)S(1)} %maximum_add_fusion), channel_id=1, source_target_pairs={{0,4},{1,5},{2,6},{3,7},{4,0},{5,1},{6,2},{7,3},{8,12},{9,13},{10,... | collective-permute-start | bytes 73736 | tf_op jit(solution)/shard_map/ppermute | solution.py:23
  58.8 4.5 %collective-permute-start.16 = (f32[128]{0:T(128)S(1)}, f32[128]{0:T(128)S(1)}, u32[]{:S(2)}, u32[]{:S(2)}) collective-permute-start(f32[128]{0:T(128)S(1)} %select_reduce_fusion), channel_id=1, source_target_pairs={{0,8},{1,9},{2,10},{3,11},{4,12},{5,13},{6,14},{7,15},{8,0},{9,1},... | collective-permute-start | bytes 1544 | tf_op jit(solution)/shard_map/ppermute | solution.py:23
where the time goes:
time: 64.1 us; the launch traced here: 63.9 us
  waiting for transfers between devices  26.7 us (42%)
  starting transfers between devices  17.8 us (28%)
  Pallas kernels  13.9 us (22%)
  local copies, waits for them, and re-layouts  3.68 us (6%)
  other arithmetic  1.07 us (2%)
  between operations  0.76 us (1%)
    ppermute x9, waiting for transfers between devices, exchange(): return lax.ppermute(value, AXES, [(i, i ^ xor) for i in range(count)])  17.1 us
    ppermute x8, starting transfers between devices, exchange_flipped(): return lax.ppermute(value, AXES, pairs)  9.59 us
    ppermute x8, waiting for transfers between devices, exchange_flipped(): return lax.ppermute(value, AXES, pairs)  9.56 us
    pallas_call x4, Pallas kernels, far(): pl.pallas_call(functools.partial(far_kernel, count=count, width=width, ch...  9.29 us
    ppermute x9, starting transfers between devices, exchange(): return lax.ppermute(value, AXES, [(i, i ^ xor) for i in range(count)])  8.17 us
    pallas_call x1, Pallas kernels, near(): pl.pallas_call(functools.partial(near_kernel, width=width), out_shape=jax...  4.61 us
    slice x3, local copies, waits for them, and re-layouts, send(): piece = lax.slice_in_dim(source, at, at + n, axis=0)  2.17 us
  transfers between devices with their start and end apart: 17, of which 12 were waited for; matrix products, arithmetic and copies ran while one was open for 5% of the time, Pallas kernels for 18%

commit v1 on v0

v1 whole, which is shorter than its diff:
```python
import functools
import math

import jax
import jax.numpy as jnp
from jax import lax
from jax.experimental import pallas as pl
from jax.experimental.pallas import tpu as pltpu
from jax.sharding import PartitionSpec as P

CLUSTERS = 128
TAU = 25.0
LOG2E = math.log2(math.e)
AXES = ("blk", "sub")
LANES = 128
VMEM = pl.BlockSpec(memory_space=pltpu.VMEM)
SMEM = pl.BlockSpec(memory_space=pltpu.SMEM)
PARAMS = pltpu.CompilerParams(vmem_limit_bytes=16 << 20)


def exchange(value, xor):
    count = lax.axis_size("blk") * lax.axis_size("sub")
    return lax.ppermute(value, AXES, [(i, i ^ xor) for i in range(count)])


def exchange_flipped(value, chip_bit, flip):
    pairs = []
    for blk in range(lax.axis_size("blk")):
        for sub in range(2):
            source = (blk ^ (1 << chip_bit)) * 2 + (sub ^ flip(blk))
            pairs.append((source, blk * 2 + sub))
    return lax.ppermute(value, AXES, pairs)


def flip_x(blk):
    return (blk ^ (blk >> 1)) & 1


def flip_z(blk):
    return (blk >> 1) & 1


def down_rows(lab, first, size):
    pieces = []
    for at in range(first, first + size, LANES):
        n = min(LANES, first + size - at)
        pieces.append(jnp.broadcast_to(lab[:, at : at + n], (LANES, n)).T)
    return pieces[0] if len(pieces) == 1 else jnp.concatenate(pieces, axis=0)


def tile(rows, down, cols_ref, lab_ref, sum_ref, line, start, size, width, fold=True):
    scale = TAU * LOG2E / width
    folded = jnp.zeros((rows.shape[0], LANES), jnp.float32)
    for at in range(0, size, 256):
        n = min(256, size - at)
        score = lax.dot_general(
            rows, cols_ref[at : at + n, :], (((1,), (1,)), ((), ())), preferred_element_type=jnp.float32
        )
        power = jnp.exp2(score * scale - TAU * LOG2E)
        for lane in range(0, n, LANES):
            there = slice(start + at + lane, start + at + lane + LANES)
            value = jnp.where(down == lab_ref[:, there], power[:, lane : lane + LANES], 0.0)
            sum_ref[line : line + 1, there] = sum_ref[line : line + 1, there] + jnp.sum(value, axis=0, keepdims=True)
            if fold:
                folded = folded + value
    return folded


def to_lanes(folded):
    return jnp.sum(folded.T, axis=0, keepdims=True)


def split_kernel(source, *rest, spans):
    outs, sem = rest[:-1], rest[-1]
    copies = [
        pltpu.make_async_copy(source.at[pl.ds(at, n)], out, sem.at[i]) for i, ((at, n), out) in enumerate(zip(spans, outs))
    ]
    for copy in copies:
        copy.start()
    for copy in copies:
        copy.wait()


def split(source, spans):
    width = source.shape[1]
    return pl.pallas_call(
        functools.partial(split_kernel, spans=tuple(spans)),
        out_shape=[jax.ShapeDtypeStruct((n, width), source.dtype) for _, n in spans],
        in_specs=[pl.BlockSpec(memory_space=pltpu.HBM)],
        out_specs=[VMEM] * len(spans),
        scratch_shapes=[pltpu.SemaphoreType.DMA((len(spans),))],
        compiler_params=PARAMS,
        cost_estimate=pl.CostEstimate(flops=0, bytes_accessed=4 * width * sum(n for _, n in spans), transcendentals=0),
    )(source)


def near_kernel(*refs, width, chunks):
    pieces = refs[: len(chunks)]
    other_ref, own_row, other_row, out_ref = refs[len(chunks) :]
    out_ref[...] = jnp.zeros_like(out_ref)
    count = sum(chunks)
    rows = [(piece, own_row, 0, at, n) for piece, at, n in zip(pieces, starts(chunks), chunks)]
    rows += [(other_ref, other_row, at, at, min(256, count - at)) for at in range(0, count, 256)]
    for ref, lab, inner, at, m in rows:
        down = down_rows(lab, at, m)
        for piece, start, n in zip(pieces, starts(chunks), chunks):
            tile(ref[inner : inner + m, :], down, piece, own_row, out_ref, 0, start, n, width, False)


def starts(chunks):
    return [sum(chunks[:k]) for k in range(len(chunks))]


def near(own, other, own_row, other_row, chunks):
    count, width = other.shape
    return pl.pallas_call(
        functools.partial(near_kernel, width=width, chunks=tuple(chunks)),
        out_shape=jax.ShapeDtypeStruct((3, count), jnp.float32),
        in_specs=[VMEM] * (len(own) + 3),
        out_specs=VMEM,
        compiler_params=PARAMS,
        cost_estimate=pl.CostEstimate(
            flops=4 * count * count * width, bytes_accessed=4 * count * width, transcendentals=2 * count * count
        ),
    )(*own, other, own_row, other_row)


def far_kernel(*refs, width, chunks, xn, zn, new):
    parts = len(chunks)
    own, refs = refs[:parts], refs[parts:]
    xs, zs = refs[:xn], refs[xn : xn + zn]
    own_row, x_row, z_row, before, sums = refs[xn + zn :]
    rows = {"x": x_row, "z": z_row}
    at = starts(chunks)
    sums[...] = before[...]
    fresh = []
    for way in new:
        k = (xn if way == "x" else zn) - 1
        piece = (xs if way == "x" else zs)[k]
        fresh.append((way, k, piece[...], down_rows(rows[way], at[k], chunks[k])))
    all_rows = fresh[0][2] if len(fresh) == 1 else jnp.concatenate([f[2] for f in fresh], axis=0)
    all_down = fresh[0][3] if len(fresh) == 1 else jnp.concatenate([f[3] for f in fresh], axis=0)
    fold = jnp.zeros((all_rows.shape[0], LANES), jnp.float32)
    for j in range(parts):
        fold = fold + tile(all_rows, all_down, own[j], own_row, sums, 0, at[j], chunks[j], width)
    first = 0
    for way, k, piece, down in fresh:
        mine, others, other_row, line = (1, zs, z_row, 2) if way == "x" else (2, xs, x_row, 1)
        if way == "z" and "x" in new:
            others = others[:-1]
        part = fold[first : first + chunks[k]]
        for j in range(len(others)):
            part = part + tile(piece, down, others[j], other_row, sums, line, at[j], chunks[j], width)
        there = slice(at[k], at[k] + chunks[k])
        sums[mine : mine + 1, there] = sums[mine : mine + 1, there] + to_lanes(part)
        first += chunks[k]


def far(own, xs, zs, own_row, x_row, z_row, sums, chunks, new):
    width, count = own[0].shape[1], sum(chunks)
    n = chunks[len(xs) - 1 if "x" in new else len(zs) - 1]
    pairs = n * len(new) * (count + sum(chunks[: len(xs)]))
    return pl.pallas_call(
        functools.partial(far_kernel, width=width, chunks=tuple(chunks), xn=len(xs), zn=len(zs), new=new),
        out_shape=jax.ShapeDtypeStruct(sums.shape, jnp.float32),
        in_specs=[VMEM] * (len(own) + len(xs) + len(zs) + 4),
        out_specs=VMEM,
        compiler_params=PARAMS,
        cost_estimate=pl.CostEstimate(
            flops=2 * pairs * width, bytes_accessed=2 * width * (count + sum(chunks)), transcendentals=pairs
        ),
    )(*own, *xs, *zs, own_row, x_row, z_row, sums)


CHUNKS = 4


def cut(count):
    tiles = count // LANES
    base, more = divmod(tiles - 1, CHUNKS - 1)
    return [(base + (k < more)) * LANES for k in range(CHUNKS - 1)] + [LANES]


def per_device(embeddings, labels):
    count, _ = embeddings.shape
    blk = lax.axis_index("blk")
    chunks = cut(count)
    turns = jnp.stack([flip_x(blk), flip_z(blk)]).astype(jnp.int32)
    xs, zs = [], []

    def send(piece):
        xs.append(exchange_flipped(piece, 0, flip_x))
        zs.append(exchange_flipped(piece, 1, flip_z))

    spans = list(zip(starts(chunks), chunks))
    own = split(embeddings, spans[:1])
    send(own[0])
    lab = labels[None, :]
    other = exchange(lab, 1)
    lab_s = jnp.concatenate([lab, other], axis=0)
    lab_x = exchange(lab_s, 2)
    lab_z = exchange(lab_s, 4)
    source, lab = lax.optimization_barrier((embeddings, lab))
    if len(chunks) > 1:
        own = own + split(source, spans[1:])
    for k in range(1, len(chunks)):
        send(own[k])
    lab_d = exchange(lab_x, 4)
    partner = exchange(source, 1)
    lab_all = jnp.concatenate([lab_s, lab_x, lab_z, lab_d], axis=0)
    x_lab = jnp.where(turns[0] == 1, lab_x[1:2], lab_x[0:1])
    z_lab = jnp.where(turns[1] == 1, lab_z[1:2], lab_z[0:1])
    sums = near(own, partner, lab, other, chunks)
    last = len(chunks)
    for k in range(1, last):
        sums = far(own, xs[:k], zs[:k], lab, x_lab, z_lab, sums, chunks, "xz")
    sums = far(own, xs, zs[:-1], lab, x_lab, z_lab, sums, chunks, "x")
    sums = far(own, xs, zs, lab, x_lab, z_lab, sums, chunks, "z")
    ax, bz = turns[0] == 1, turns[1] == 1
    part = spread3(sums, ax, bz) + turned(spread3(exchange(sums, 3), ~ax, bz), 3)
    six = jnp.concatenate([part[0:4], jnp.where(bz, part[5:6], part[4:5]), jnp.where(bz, part[6:7], part[7:8])], axis=0)
    part = part + turned(spread6(exchange(six, 5), ~bz), 5)
    part = part + turned(exchange(part, 1), 1)
    weight = 1.0 / part
    ident = jnp.arange(CLUSTERS, dtype=jnp.int32)
    mass = jnp.sum(jnp.where(lab_all[:, None, :] == ident[None, :, None], weight[:, None, :], 0.0), axis=(0, 2))
    bit = 8
    while bit < lax.axis_size("blk") * 2:
        mass = mass + exchange(mass, bit + 1)
        bit *= 2
    return weight[0], mass


def turned(rows, xor):
    return jnp.concatenate([rows[r ^ xor : (r ^ xor) + 1] for r in range(8)], axis=0)


def spread3(sums, ax, bz):
    own, x, z = sums[0:1], sums[1:2], sums[2:3]
    zero = jnp.zeros_like(own)
    return jnp.concatenate(
        [own, zero, jnp.where(ax, zero, x), jnp.where(ax, x, zero), jnp.where(bz, zero, z), jnp.where(bz, z, zero), zero, zero],
        axis=0,
    )


def spread6(six, bz):
    z, d = six[4:5], six[5:6]
    zero = jnp.zeros_like(z)
    return jnp.concatenate(
        [six[0:4], jnp.where(bz, zero, z), jnp.where(bz, z, zero), jnp.where(bz, d, zero), jnp.where(bz, zero, d)], axis=0
    )


def solution(mesh):
    in_specs = (P(("parts", "blk", "sub"), None), P(("parts", "blk", "sub")))
    out_specs = (P(("parts", "blk", "sub")), P("parts"))
    return jax.shard_map(per_device, mesh=mesh, in_specs=in_specs, out_specs=out_specs, check_vma=False)
```

time: 64.1 us -> 65.1 us (1.016)
  starting transfers between devices: 17.8 us -> 20.2 us
  Pallas kernels: 13.9 us -> 13 us
  local copies, waits for them, and re-layouts: 3.68 us -> 2.97 us
    ppermute x9, starting transfers between devices: 8.17 us -> 10.7 us  [exchange(): return lax.ppermute(value, AXES, [(i, i ^ xor) for i in range(count)])]
    slice x6 -> x2, local copies, waits for them, and re-layouts: 2.21 us -> 0.02 us  [the longest x1 0.02 us: turned(): rows[r ^ xor:(r ^ xor) + 1]]
    ppermute x9, waiting for transfers between devices: 17.1 us -> 19 us  [exchange(): return lax.ppermute(value, AXES, [(i, i ^ xor) for i in range(count)])]
    ppermute x8, waiting for transfers between devices: 9.56 us -> 7.87 us  [exchange_flipped(): return lax.ppermute(value, AXES, pairs)]
    unnamed x2, local copies, waits for them, and re-layouts: 0.01 us -> 1.41 us
    pallas_call x5 -> x8, Pallas kernels: 13.9 us -> 13 us  [the longest x5 7.27 us: far(): pl.pallas_call(functools.partial(far_kernel, width=width, chunks=tuple(ch...]
  transfers between devices with their start and end apart: 17 -> 17, of which waited for: 12 -> 9; matrix products, arithmetic and copies ran while one was open for 5% -> 1% of each run, Pallas kernels for 18% -> 18%
where the time goes in v1:
time: 65.1 us; the launch traced here: 64.9 us
  waiting for transfers between devices  26.8 us (41%)
  starting transfers between devices  20.2 us (31%)
  Pallas kernels  13 us (20%)
  local copies, waits for them, and re-layouts  2.97 us (5%)
  other arithmetic  1.02 us (2%)
  between operations  0.8 us (1%)
    ppermute x9, waiting for transfers between devices, exchange(): return lax.ppermute(value, AXES, [(i, i ^ xor) for i in range(count)])  19 us
    ppermute x9, starting transfers between devices, exchange(): return lax.ppermute(value, AXES, [(i, i ^ xor) for i in range(count)])  10.7 us
    ppermute x8, starting transfers between devices, exchange_flipped(): return lax.ppermute(value, AXES, pairs)  9.48 us
    ppermute x8, waiting for transfers between devices, exchange_flipped(): return lax.ppermute(value, AXES, pairs)  7.87 us
    pallas_call x5, Pallas kernels, far(): pl.pallas_call(functools.partial(far_kernel, width=width, chunks=tuple(ch...  7.27 us
    pallas_call x1, Pallas kernels, near(): pl.pallas_call(functools.partial(near_kernel, width=width, chunks=tuple(c...  5.6 us
    unnamed x2, local copies, waits for them, and re-layouts  1.41 us
  transfers between devices with their start and end apart: 17, of which 9 were waited for; matrix products, arithmetic and copies ran while one was open for 1% of the time, Pallas kernels for 18%

profile of v1, /device:TPU:0, one launch (start us, length us, event | category | flops | bytes accessed | tf_op | source)
XLA Modules:
  0.0 64.9 jit_solution(10137844669170761479)
XLA Ops:
  0.6 0.7 %broadcast_in_dim.18.refs_5_.refs_6_.refs_8_.refs_10_.refs_11_.refs_12_ = s32[1,768]{1,0:T(1,128)S(1)} reshape(s32[768]{0:T(1024)} %param.3) | data formatting | bytes 6144 | tf_op jit(solution)/shard_map/broadcast_in_dim | solution.py:198
  1.3 0.5 collective-permute-start.11
  1.8 1.4 %copy-done = bf16[768,1024]{1,0:T(8,128)(2,1)S(1)} copy-done((bf16[768,1024]{1,0:T(8,128)(2,1)S(1)}, bf16[768,1024]{1,0:T(8,128)(2,1)}, u32[]{:S(2)}) %copy-start) | copy-done | bytes 1572888
  3.3 2.6 %collective-permute-start = (bf16[256,1024]{1,0:T(8,128)(2,1)S(1)}, bf16[256,1024]{1,0:T(8,128)(2,1)S(1)}, u32[]{:S(2)}, u32[]{:S(2)}) collective-permute-start(bf16[256,1024]{1,0:T(8,128)(2,1)S(1)} %shard_map.41.refs_0_), channel_id=1, source_target_pairs={{2,0},{3,1},{1,2},{0,3},{7,4},{6,5},{4,6},{5,7},{10,8},{11,9},{9,1... | collective-permute-start | bytes 1572872 | tf_op jit(solution)/shard_map/ppermute | solution.py:32
  5.9 2.2 %collective-permute-start.9 = (s32[2,768]{1,0:T(2,128)S(1)}, s32[2,768]{1,0:T(2,128)S(1)}, u32[]{:S(2)}, u32[]{:S(2)}) collective-permute-start(s32[2,768]{1,0:T(2,128)S(1)} %pad_add_fusion), channel_id=1, source_target_pairs={{0,2},{1,3},{2,0},{3,1},{4,6},{5,7},{6,4},{7,5},{8,10},{9,11},{10,... | collective-permute-start | bytes 18440 | tf_op jit(solution)/shard_map/ppermute | solution.py:23
  8.1 1.0 %collective-permute-start.4 = (bf16[256,1024]{1,0:T(8,128)(2,1)S(1)}, bf16[256,1024]{1,0:T(8,128)(2,1)S(1)}, u32[]{:S(2)}, u32[]{:S(2)}) collective-permute-start(bf16[256,1024]{1,0:T(8,128)(2,1)S(1)} %shard_map.41.refs_0_), channel_id=1, source_target_pairs={{4,0},{5,1},{6,2},{7,3},{1,4},{0,5},{3,6},{2,7},{12,8},{13,9},{14,... | collective-permute-start | bytes 1572872 | tf_op jit(solution)/shard_map/ppermute | solution.py:32
  9.3 0.8 %collective-permute-start.1 = (bf16[256,1024]{1,0:T(8,128)(2,1)S(1)}, bf16[256,1024]{1,0:T(8,128)(2,1)S(1)}, u32[]{:S(2)}, u32[]{:S(2)}) collective-permute-start(bf16[256,1024]{1,0:T(8,128)(2,1)S(1)} %get-tuple-element.8.refs_1_), channel_id=1, source_target_pairs={{2,0},{3,1},{1,2},{0,3},{7,4},{6,5},{4,6},{5,7},{10,8},{11,9},{9,1... | collective-permute-start | bytes 1572872 | tf_op jit(solution)/shard_map/ppermute | solution.py:32
  10.1 9.1 %collective-permute-done.9 = s32[2,768]{1,0:T(2,128)S(1)} collective-permute-done((s32[2,768]{1,0:T(2,128)S(1)}, s32[2,768]{1,0:T(2,128)S(1)}, u32[]{:S(2)}, u32[]{:S(2)}) %collective-permute-start.9) | collective-permute-done | bytes 6176 | tf_op jit(solution)/shard_map/ppermute | solution.py:23
  19.2 1.7 %collective-permute-start.10 = (s32[2,768]{1,0:T(2,128)S(1)}, s32[2,768]{1,0:T(2,128)S(1)}, u32[]{:S(2)}, u32[]{:S(2)}) collective-permute-start(s32[2,768]{1,0:T(2,128)S(1)} %pad_add_fusion), channel_id=1, source_target_pairs={{0,4},{1,5},{2,6},{3,7},{4,0},{5,1},{6,2},{7,3},{8,12},{9,13},{10,... | collective-permute-start | bytes 18440 | tf_op jit(solution)/shard_map/ppermute | solution.py:23
  20.9 1.9 %collective-permute-done.10 = s32[2,768]{1,0:T(2,128)S(1)} collective-permute-done((s32[2,768]{1,0:T(2,128)S(1)}, s32[2,768]{1,0:T(2,128)S(1)}, u32[]{:S(2)}, u32[]{:S(2)}) %collective-permute-start.10) | collective-permute-done | bytes 6176 | tf_op jit(solution)/shard_map/ppermute | solution.py:23
  22.9 0.9 %collective-permute-start.5 = (bf16[256,1024]{1,0:T(8,128)(2,1)S(1)}, bf16[256,1024]{1,0:T(8,128)(2,1)S(1)}, u32[]{:S(2)}, u32[]{:S(2)}) collective-permute-start(bf16[256,1024]{1,0:T(8,128)(2,1)S(1)} %get-tuple-element.8.refs_1_), channel_id=1, source_target_pairs={{4,0},{5,1},{6,2},{7,3},{1,4},{0,5},{3,6},{2,7},{12,8},{13,9},{14,... | collective-permute-start | bytes 1572872 | tf_op jit(solution)/shard_map/ppermute | solution.py:32
  23.7 2.5 %collective-permute-start.2 = (bf16[128,1024]{1,0:T(8,128)(2,1)S(1)}, bf16[128,1024]{1,0:T(8,128)(2,1)S(1)}, u32[]{:S(2)}, u32[]{:S(2)}) collective-permute-start(bf16[128,1024]{1,0:T(8,128)(2,1)S(1)} %get-tuple-element.9.refs_2_), channel_id=1, source_target_pairs={{2,0},{3,1},{1,2},{0,3},{7,4},{6,5},{4,6},{5,7},{10,8},{11,9},{9,1... | collective-permute-start | bytes 786440 | tf_op jit(solution)/shard_map/ppermute | solution.py:32
  26.2 5.6 %shard_map.43.refs_9_ = f32[3,768]{1,0:T(4,128)S(1)} custom-call(bf16[256,1024]{1,0:T(8,128)(2,1)S(1)} %shard_map.41.refs_0_, bf16[256,1024]{1,0:T(8,128)(2,1)S(1)} %get-tuple-element.8.refs_1_, bf16[128,1024]{1,0:T(8,128)(2,1)S(1)} %get-tuple-element.9.refs_2_, bf16[128,1024]{1,0:T(8,128)(2,1)S(1)} %get-tuple-element.10.refs_3_, ...), custom_call_target="tpu_custom_call" | custom-call | flops 2415919104 | bytes 3145728 | tf_op jit(solution)/shard_map/pallas_call | solution.py:116
  32.1 1.4 %collective-permute-start.7 = (bf16[128,1024]{1,0:T(8,128)(2,1)S(1)}, bf16[128,1024]{1,0:T(8,128)(2,1)S(1)}, u32[]{:S(2)}, u32[]{:S(2)}) collective-permute-start(bf16[128,1024]{1,0:T(8,128)(2,1)S(1)} %get-tuple-element.10.refs_3_), channel_id=1, source_target_pairs={{4,0},{5,1},{6,2},{7,3},{1,4},{0,5},{3,6},{2,7},{12,8},{13,9},{14,... | collective-permute-start | bytes 786440 | tf_op jit(solution)/shard_map/ppermute | solution.py:32
  33.5 1.6 %shard_map.44.refs_11_ = f32[3,768]{1,0:T(4,128)S(1)} custom-call(bf16[256,1024]{1,0:T(8,128)(2,1)S(1)} %shard_map.41.refs_0_, bf16[256,1024]{1,0:T(8,128)(2,1)S(1)} %get-tuple-element.8.refs_1_, bf16[128,1024]{1,0:T(8,128)(2,1)S(1)} %get-tuple-element.9.refs_2_, bf16[128,1024]{1,0:T(8,128)(2,1)S(1)} %get-tuple-element.10.refs_3_, ...), custom_call_target="tpu_custom_call" | custom-call | flops 1073741824 | bytes 3145728 | tf_op jit(solution)/shard_map/pallas_call | solution.py:163
  35.0 2.6 %collective-permute-done.5.refs_7_.refs_8_.refs_9_ = bf16[256,1024]{1,0:T(8,128)(2,1)S(1)} collective-permute-done((bf16[256,1024]{1,0:T(8,128)(2,1)S(1)}, bf16[256,1024]{1,0:T(8,128)(2,1)S(1)}, u32[]{:S(2)}, u32[]{:S(2)}) %collective-permute-start.5) | collective-permute-done | bytes 524320 | tf_op jit(solution)/shard_map/ppermute | solution.py:32
  37.6 1.9 %shard_map.45.refs_13_ = f32[3,768]{1,0:T(4,128)S(1)} custom-call(bf16[256,1024]{1,0:T(8,128)(2,1)S(1)} %shard_map.41.refs_0_, bf16[256,1024]{1,0:T(8,128)(2,1)S(1)} %get-tuple-element.8.refs_1_, bf16[128,1024]{1,0:T(8,128)(2,1)S(1)} %get-tuple-element.9.refs_2_, bf16[128,1024]{1,0:T(8,128)(2,1)S(1)} %get-tuple-element.10.refs_3_, ...), custom_call_target="tpu_custom_call" | custom-call | flops 1342177280 | bytes 3145728 | tf_op jit(solution)/shard_map/pallas_call | solution.py:163
  39.5 3.7 %collective-permute-done.6.refs_9_.refs_10_ = bf16[128,1024]{1,0:T(8,128)(2,1)S(1)} collective-permute-done((bf16[128,1024]{1,0:T(8,128)(2,1)S(1)}, bf16[128,1024]{1,0:T(8,128)(2,1)S(1)}, u32[]{:S(2)}, u32[]{:S(2)}) %collective-permute-start.6) | collective-permute-done | bytes 262176 | tf_op jit(solution)/shard_map/ppermute | solution.py:32
  43.3 1.5 %shard_map.46.refs_14_ = f32[3,768]{1,0:T(4,128)S(1)} custom-call(bf16[256,1024]{1,0:T(8,128)(2,1)S(1)} %shard_map.41.refs_0_, bf16[256,1024]{1,0:T(8,128)(2,1)S(1)} %get-tuple-element.8.refs_1_, bf16[128,1024]{1,0:T(8,128)(2,1)S(1)} %get-tuple-element.9.refs_2_, bf16[128,1024]{1,0:T(8,128)(2,1)S(1)} %get-tuple-element.10.refs_3_, ...), custom_call_target="tpu_custom_call" | custom-call | flops 738197504 | bytes 3145728 | tf_op jit(solution)/shard_map/pallas_call | solution.py:163
  44.8 1.1 %shard_map.47.refs_15_ = f32[3,768]{1,0:T(4,128)S(1)} custom-call(bf16[256,1024]{1,0:T(8,128)(2,1)S(1)} %shard_map.41.refs_0_, bf16[256,1024]{1,0:T(8,128)(2,1)S(1)} %get-tuple-element.8.refs_1_, bf16[128,1024]{1,0:T(8,128)(2,1)S(1)} %get-tuple-element.9.refs_2_, bf16[128,1024]{1,0:T(8,128)(2,1)S(1)} %get-tuple-element.10.refs_3_, ...), custom_call_target="tpu_custom_call" | custom-call | flops 402653184 | bytes 3145728 | tf_op jit(solution)/shard_map/pallas_call | solution.py:163
  45.9 1.5 %collective-permute-done.7.refs_11_ = bf16[128,1024]{1,0:T(8,128)(2,1)S(1)} collective-permute-done((bf16[128,1024]{1,0:T(8,128)(2,1)S(1)}, bf16[128,1024]{1,0:T(8,128)(2,1)S(1)}, u32[]{:S(2)}, u32[]{:S(2)}) %collective-permute-start.7) | collective-permute-done | bytes 262176 | tf_op jit(solution)/shard_map/ppermute | solution.py:32
  47.4 1.2 %shard_map.48 = f32[3,768]{1,0:T(4,128)S(1)} custom-call(bf16[256,1024]{1,0:T(8,128)(2,1)S(1)} %shard_map.41.refs_0_, bf16[256,1024]{1,0:T(8,128)(2,1)S(1)} %get-tuple-element.8.refs_1_, bf16[128,1024]{1,0:T(8,128)(2,1)S(1)} %get-tuple-element.9.refs_2_, bf16[128,1024]{1,0:T(8,128)(2,1)S(1)} %get-tuple-element.10.refs_3_, ...), custom_call_target="tpu_custom_call" | custom-call | flops 402653184 | bytes 3145728 | tf_op jit(solution)/shard_map/pallas_call | solution.py:163
  49.1 2.7 %collective-permute-done.12 = f32[3,768]{1,0:T(4,128)S(1)} collective-permute-done((f32[3,768]{1,0:T(4,128)S(1)}, f32[3,768]{1,0:T(4,128)S(1)}, u32[]{:S(2)}, u32[]{:S(2)}) %collective-permute-start.12) | collective-permute-done | bytes 9248 | tf_op jit(solution)/shard_map/ppermute | solution.py:23
  51.9 2.2 %collective-permute-start.13 = (f32[6,768]{1,0:T(8,128)S(1)}, f32[6,768]{1,0:T(8,128)S(1)}, u32[]{:S(2)}, u32[]{:S(2)}) collective-permute-start(f32[6,768]{1,0:T(8,128)S(1)} %pad_maximum_fusion), channel_id=1, source_target_pairs={{0,5},{1,4},{2,7},{3,6},{4,1},{5,0},{6,3},{7,2},{8,13},{9,12},{10,... | collective-permute-start | bytes 55304 | tf_op jit(solution)/shard_map/ppermute | solution.py:23
  54.2 1.5 %collective-permute-done.13 = f32[6,768]{1,0:T(8,128)S(1)} collective-permute-done((f32[6,768]{1,0:T(8,128)S(1)}, f32[6,768]{1,0:T(8,128)S(1)}, u32[]{:S(2)}, u32[]{:S(2)}) %collective-permute-start.13) | collective-permute-done | bytes 18464 | tf_op jit(solution)/shard_map/ppermute | solution.py:23
  55.8 0.5 collective-permute-start.14
  56.2 1.7 %collective-permute-start.15 = (s32[2,768]{1,0:T(2,128)S(1)}, s32[2,768]{1,0:T(2,128)S(1)}, u32[]{:S(2)}, u32[]{:S(2)}) collective-permute-start(s32[2,768]{1,0:T(2,128)S(1)} %collective-permute-done.9), channel_id=1, source_target_pairs={{0,4},{1,5},{2,6},{3,7},{4,0},{5,1},{6,2},{7,3},{8,12},{9,13},{10,... | collective-permute-start | bytes 18440 | tf_op jit(solution)/shard_map/ppermute | solution.py:23
  58.0 1.9 %collective-permute-done.15 = s32[2,768]{1,0:T(2,128)S(1)} collective-permute-done((s32[2,768]{1,0:T(2,128)S(1)}, s32[2,768]{1,0:T(2,128)S(1)}, u32[]{:S(2)}, u32[]{:S(2)}) %collective-permute-start.15) | collective-permute-done | bytes 6176 | tf_op jit(solution)/shard_map/ppermute | solution.py:23
  60.4 1.5 %collective-permute-start.16 = (f32[128]{0:T(128)S(1)}, f32[128]{0:T(128)S(1)}, u32[]{:S(2)}, u32[]{:S(2)}) collective-permute-start(f32[128]{0:T(128)S(1)} %select_reduce_fusion), channel_id=1, source_target_pairs={{0,9},{1,8},{2,11},{3,10},{4,13},{5,12},{6,15},{7,14},{8,1},{9,0},... | collective-permute-start | bytes 1544 | tf_op jit(solution)/shard_map/ppermute | solution.py:23
  61.9 0.6 slice_reduce_fusion
  62.5 1.8 %collective-permute-done.16 = f32[128]{0:T(128)S(1)} collective-permute-done((f32[128]{0:T(128)S(1)}, f32[128]{0:T(128)S(1)}, u32[]{:S(2)}, u32[]{:S(2)}) %collective-permute-start.16) | collective-permute-done | bytes 544 | tf_op jit(solution)/shard_map/ppermute | solution.py:23
  64.3 0.5 add.27
  (36 shorter events, 1.6 us)
Async XLA Ops:
  1.3 24.9 %collective-permute-start.11 = (bf16[768,1024]{1,0:T(8,128)(2,1)}, bf16[768,1024]{1,0:T(8,128)(2,1)}, u32[]{:S(2)}, u32[]{:S(2)}) collective-permute-start(bf16[768,1024]{1,0:T(8,128)(2,1)} %source.2), channel_id=1, source_target_pairs={{0,1},{1,0},{2,3},{3,2},{4,5},{5,4},{6,7},{7,6},{8,9},{9,8},{10,11... | collective-permute-start | bytes 4718600 | tf_op jit(solution)/shard_map/ppermute | solution.py:23
  1.8 4.1 %collective-permute-start.8 = (s32[1,768]{1,0:T(1,128)S(1)}, s32[1,768]{1,0:T(1,128)S(1)}, u32[]{:S(2)}, u32[]{:S(2)}) collective-permute-start(s32[1,768]{1,0:T(1,128)S(1)} %broadcast_in_dim.18.refs_5_.refs_6_.refs_8_.refs_10_.refs_11_.refs_12_), channel_id=1, source_target_pairs={{0,1},{1,0},{2,3},{3,2},{4,5},{5,4},{6,7},{7,6},{8,9},{9,8},{10,11... | collective-permute-start | bytes 9224 | tf_op jit(solution)/shard_map/ppermute | solution.py:23
  1.8 1.4 %copy-start = (bf16[768,1024]{1,0:T(8,128)(2,1)S(1)}, bf16[768,1024]{1,0:T(8,128)(2,1)}, u32[]{:S(2)}) copy-start(bf16[768,1024]{1,0:T(8,128)(2,1)} %source.2) | copy-start | bytes 4718596
  3.3 20.4 %collective-permute-start = (bf16[256,1024]{1,0:T(8,128)(2,1)S(1)}, bf16[256,1024]{1,0:T(8,128)(2,1)S(1)}, u32[]{:S(2)}, u32[]{:S(2)}) collective-permute-start(bf16[256,1024]{1,0:T(8,128)(2,1)S(1)} %shard_map.41.refs_0_), channel_id=1, source_target_pairs={{2,0},{3,1},{1,2},{0,3},{7,4},{6,5},{4,6},{5,7},{10,8},{11,9},{9,1... | collective-permute-start | bytes 1572872 | tf_op jit(solution)/shard_map/ppermute | solution.py:32
  5.9 13.3 %collective-permute-start.9 = (s32[2,768]{1,0:T(2,128)S(1)}, s32[2,768]{1,0:T(2,128)S(1)}, u32[]{:S(2)}, u32[]{:S(2)}) collective-permute-start(s32[2,768]{1,0:T(2,128)S(1)} %pad_add_fusion), channel_id=1, source_target_pairs={{0,2},{1,3},{2,0},{3,1},{4,6},{5,7},{6,4},{7,5},{8,10},{9,11},{10,... | collective-permute-start | bytes 18440 | tf_op jit(solution)/shard_map/ppermute | solution.py:23
  8.1 23.7 %collective-permute-start.4 = (bf16[256,1024]{1,0:T(8,128)(2,1)S(1)}, bf16[256,1024]{1,0:T(8,128)(2,1)S(1)}, u32[]{:S(2)}, u32[]{:S(2)}) collective-permute-start(bf16[256,1024]{1,0:T(8,128)(2,1)S(1)} %shard_map.41.refs_0_), channel_id=1, source_target_pairs={{4,0},{5,1},{6,2},{7,3},{1,4},{0,5},{3,6},{2,7},{12,8},{13,9},{14,... | collective-permute-start | bytes 1572872 | tf_op jit(solution)/shard_map/ppermute | solution.py:32
  9.3 22.8 %collective-permute-start.1 = (bf16[256,1024]{1,0:T(8,128)(2,1)S(1)}, bf16[256,1024]{1,0:T(8,128)(2,1)S(1)}, u32[]{:S(2)}, u32[]{:S(2)}) collective-permute-start(bf16[256,1024]{1,0:T(8,128)(2,1)S(1)} %get-tuple-element.8.refs_1_), channel_id=1, source_target_pairs={{2,0},{3,1},{1,2},{0,3},{7,4},{6,5},{4,6},{5,7},{10,8},{11,9},{9,1... | collective-permute-start | bytes 1572872 | tf_op jit(solution)/shard_map/ppermute | solution.py:32
  19.2 3.6 %collective-permute-start.10 = (s32[2,768]{1,0:T(2,128)S(1)}, s32[2,768]{1,0:T(2,128)S(1)}, u32[]{:S(2)}, u32[]{:S(2)}) collective-permute-start(s32[2,768]{1,0:T(2,128)S(1)} %pad_add_fusion), channel_id=1, source_target_pairs={{0,4},{1,5},{2,6},{3,7},{4,0},{5,1},{6,2},{7,3},{8,12},{9,13},{10,... | collective-permute-start | bytes 18440 | tf_op jit(solution)/shard_map/ppermute | solution.py:23
  22.9 14.8 %collective-permute-start.5 = (bf16[256,1024]{1,0:T(8,128)(2,1)S(1)}, bf16[256,1024]{1,0:T(8,128)(2,1)S(1)}, u32[]{:S(2)}, u32[]{:S(2)}) collective-permute-start(bf16[256,1024]{1,0:T(8,128)(2,1)S(1)} %get-tuple-element.8.refs_1_), channel_id=1, source_target_pairs={{4,0},{5,1},{6,2},{7,3},{1,4},{0,5},{3,6},{2,7},{12,8},{13,9},{14,... | collective-permute-start | bytes 1572872 | tf_op jit(solution)/shard_map/ppermute | solution.py:32
  23.7 15.8 %collective-permute-start.2 = (bf16[128,1024]{1,0:T(8,128)(2,1)S(1)}, bf16[128,1024]{1,0:T(8,128)(2,1)S(1)}, u32[]{:S(2)}, u32[]{:S(2)}) collective-permute-start(bf16[128,1024]{1,0:T(8,128)(2,1)S(1)} %get-tuple-element.9.refs_2_), channel_id=1, source_target_pairs={{2,0},{3,1},{1,2},{0,3},{7,4},{6,5},{4,6},{5,7},{10,8},{11,9},{9,1... | collective-permute-start | bytes 786440 | tf_op jit(solution)/shard_map/ppermute | solution.py:32
  26.2 17.0 %collective-permute-start.6 = (bf16[128,1024]{1,0:T(8,128)(2,1)S(1)}, bf16[128,1024]{1,0:T(8,128)(2,1)S(1)}, u32[]{:S(2)}, u32[]{:S(2)}) collective-permute-start(bf16[128,1024]{1,0:T(8,128)(2,1)S(1)} %get-tuple-element.9.refs_2_), channel_id=1, source_target_pairs={{4,0},{5,1},{6,2},{7,3},{1,4},{0,5},{3,6},{2,7},{12,8},{13,9},{14,... | collective-permute-start | bytes 786440 | tf_op jit(solution)/shard_map/ppermute | solution.py:32
  31.9 13.0 %collective-permute-start.3 = (bf16[128,1024]{1,0:T(8,128)(2,1)S(1)}, bf16[128,1024]{1,0:T(8,128)(2,1)S(1)}, u32[]{:S(2)}, u32[]{:S(2)}) collective-permute-start(bf16[128,1024]{1,0:T(8,128)(2,1)S(1)} %get-tuple-element.10.refs_3_), channel_id=1, source_target_pairs={{2,0},{3,1},{1,2},{0,3},{7,4},{6,5},{4,6},{5,7},{10,8},{11,9},{9,1... | collective-permute-start | bytes 786440 | tf_op jit(solution)/shard_map/ppermute | solution.py:32
  32.1 15.4 %collective-permute-start.7 = (bf16[128,1024]{1,0:T(8,128)(2,1)S(1)}, bf16[128,1024]{1,0:T(8,128)(2,1)S(1)}, u32[]{:S(2)}, u32[]{:S(2)}) collective-permute-start(bf16[128,1024]{1,0:T(8,128)(2,1)S(1)} %get-tuple-element.10.refs_3_), channel_id=1, source_target_pairs={{4,0},{5,1},{6,2},{7,3},{1,4},{0,5},{3,6},{2,7},{12,8},{13,9},{14,... | collective-permute-start | bytes 786440 | tf_op jit(solution)/shard_map/ppermute | solution.py:32
  48.6 3.2 %collective-permute-start.12 = (f32[3,768]{1,0:T(4,128)S(1)}, f32[3,768]{1,0:T(4,128)S(1)}, u32[]{:S(2)}, u32[]{:S(2)}) collective-permute-start(f32[3,768]{1,0:T(4,128)S(1)} %shard_map.48), channel_id=1, source_target_pairs={{0,3},{1,2},{2,1},{3,0},{4,7},{5,6},{6,5},{7,4},{8,11},{9,10},{10,... | collective-permute-start | bytes 27656 | tf_op jit(solution)/shard_map/ppermute | solution.py:23
  51.9 3.7 %collective-permute-start.13 = (f32[6,768]{1,0:T(8,128)S(1)}, f32[6,768]{1,0:T(8,128)S(1)}, u32[]{:S(2)}, u32[]{:S(2)}) collective-permute-start(f32[6,768]{1,0:T(8,128)S(1)} %pad_maximum_fusion), channel_id=1, source_target_pairs={{0,5},{1,4},{2,7},{3,6},{4,1},{5,0},{6,3},{7,2},{8,13},{9,12},{10,... | collective-permute-start | bytes 55304 | tf_op jit(solution)/shard_map/ppermute | solution.py:23
  55.8 4.1 %collective-permute-start.14 = (f32[8,768]{1,0:T(8,128)S(1)}, f32[8,768]{1,0:T(8,128)S(1)}, u32[]{:S(2)}, u32[]{:S(2)}) collective-permute-start(f32[8,768]{1,0:T(8,128)S(1)} %add.25), channel_id=1, source_target_pairs={{0,1},{1,0},{2,3},{3,2},{4,5},{5,4},{6,7},{7,6},{8,9},{9,8},{10,11... | collective-permute-start | bytes 73736 | tf_op jit(solution)/shard_map/ppermute | solution.py:23
  56.2 3.6 %collective-permute-start.15 = (s32[2,768]{1,0:T(2,128)S(1)}, s32[2,768]{1,0:T(2,128)S(1)}, u32[]{:S(2)}, u32[]{:S(2)}) collective-permute-start(s32[2,768]{1,0:T(2,128)S(1)} %collective-permute-done.9), channel_id=1, source_target_pairs={{0,4},{1,5},{2,6},{3,7},{4,0},{5,1},{6,2},{7,3},{8,12},{9,13},{10,... | collective-permute-start | bytes 18440 | tf_op jit(solution)/shard_map/ppermute | solution.py:23
  60.4 4.0 %collective-permute-start.16 = (f32[128]{0:T(128)S(1)}, f32[128]{0:T(128)S(1)}, u32[]{:S(2)}, u32[]{:S(2)}) collective-permute-start(f32[128]{0:T(128)S(1)} %select_reduce_fusion), channel_id=1, source_target_pairs={{0,9},{1,8},{2,11},{3,10},{4,13},{5,12},{6,15},{7,14},{8,1},{9,0},... | collective-permute-start | bytes 1544 | tf_op jit(solution)/shard_map/ppermute | solution.py:23

commit v2 on v1

v2 whole, which is shorter than its diff:
```python
import functools
import math

import jax
import jax.numpy as jnp
from jax import lax
from jax.experimental import pallas as pl
from jax.experimental.pallas import tpu as pltpu
from jax.sharding import PartitionSpec as P

CLUSTERS = 128
TAU = 25.0
LOG2E = math.log2(math.e)
AXES = ("blk", "sub")
LANES = 128
VMEM = pl.BlockSpec(memory_space=pltpu.VMEM)
SMEM = pl.BlockSpec(memory_space=pltpu.SMEM)
PARAMS = pltpu.CompilerParams(vmem_limit_bytes=16 << 20)


def exchange(value, xor):
    count = lax.axis_size("blk") * lax.axis_size("sub")
    return lax.ppermute(value, AXES, [(i, i ^ xor) for i in range(count)])


def exchange_mixed(value):
    count = lax.axis_size("blk") * lax.axis_size("sub")
    return lax.ppermute(value, AXES, [(i, i ^ 2 if i & 1 else i ^ 4) for i in range(count)])


def down_rows(lab, first, size):
    pieces = []
    for at in range(first, first + size, LANES):
        n = min(LANES, first + size - at)
        pieces.append(jnp.broadcast_to(lab[:, at : at + n], (LANES, n)).T)
    return pieces[0] if len(pieces) == 1 else jnp.concatenate(pieces, axis=0)


def tile(rows, down, cols_ref, lab_ref, sum_ref, line, start, size, width, fold=True):
    scale = TAU * LOG2E / width
    folded = jnp.zeros((rows.shape[0], LANES), jnp.float32)
    for at in range(0, size, 256):
        n = min(256, size - at)
        score = lax.dot_general(
            rows, cols_ref[at : at + n, :], (((1,), (1,)), ((), ())), preferred_element_type=jnp.float32
        )
        power = jnp.exp2(score * scale - TAU * LOG2E)
        for lane in range(0, n, LANES):
            there = slice(start + at + lane, start + at + lane + LANES)
            value = jnp.where(down == lab_ref[:, there], power[:, lane : lane + LANES], 0.0)
            sum_ref[line : line + 1, there] = sum_ref[line : line + 1, there] + jnp.sum(value, axis=0, keepdims=True)
            if fold:
                folded = folded + value
    return folded


def to_lanes(folded):
    return jnp.sum(folded.T, axis=0, keepdims=True)


def split_kernel(source, *rest, spans):
    outs, sem = rest[:-1], rest[-1]
    copies = [
        pltpu.make_async_copy(source.at[pl.ds(at, n)], out, sem.at[i]) for i, ((at, n), out) in enumerate(zip(spans, outs))
    ]
    for copy in copies:
        copy.start()
    for copy in copies:
        copy.wait()


def split(source, spans):
    width = source.shape[1]
    return pl.pallas_call(
        functools.partial(split_kernel, spans=tuple(spans)),
        out_shape=[jax.ShapeDtypeStruct((n, width), source.dtype) for _, n in spans],
        in_specs=[pl.BlockSpec(memory_space=pltpu.HBM)],
        out_specs=[VMEM] * len(spans),
        scratch_shapes=[pltpu.SemaphoreType.DMA((len(spans),))],
        compiler_params=PARAMS,
        cost_estimate=pl.CostEstimate(flops=0, bytes_accessed=4 * width * sum(n for _, n in spans), transcendentals=0),
    )(source)


def near_kernel(*refs, width, chunks):
    parts = len(chunks)
    own, other = refs[:parts], refs[parts : 2 * parts]
    own_row, other_row, out_ref = refs[2 * parts :]
    out_ref[...] = jnp.zeros_like(out_ref)
    for pieces, lab in ((own, own_row), (other, other_row)):
        for rows, first, m in zip(pieces, starts(chunks), chunks):
            down = down_rows(lab, first, m)
            for piece, at, n in zip(own, starts(chunks), chunks):
                tile(rows[...], down, piece, own_row, out_ref, 0, at, n, width, False)


def starts(chunks):
    return [sum(chunks[:k]) for k in range(len(chunks))]


def near(own, other, own_row, other_row, chunks):
    width, count = own[0].shape[1], sum(chunks)
    return pl.pallas_call(
        functools.partial(near_kernel, width=width, chunks=tuple(chunks)),
        out_shape=jax.ShapeDtypeStruct((6, count), jnp.float32),
        in_specs=[VMEM] * (2 * len(own) + 2),
        out_specs=VMEM,
        compiler_params=PARAMS,
        cost_estimate=pl.CostEstimate(
            flops=4 * count * count * width, bytes_accessed=4 * count * width, transcendentals=2 * count * count
        ),
    )(*own, *other, own_row, other_row)


_, MET_FIRST, MET_SECOND, FIRST, SECOND, CROSS = range(6)


def far_kernel(*refs, width, chunks, news, ks, groups, line):
    parts = len(chunks)
    new, refs = refs[:news], refs[news:]
    cols = [refs[parts * g : parts * (g + 1)] for g in range(len(groups))]
    refs = refs[parts * len(groups) :]
    new_row, col_rows, (before, sums) = refs[0], refs[1 : 1 + len(groups)], refs[1 + len(groups) :]
    sums[...] = before[...]
    for piece, k in zip(new, ks):
        first, n = starts(chunks)[k], chunks[k]
        rows, down = piece[...], down_rows(new_row, first, n)
        fold = jnp.zeros((n, LANES), jnp.float32)
        for pieces, lab, met in zip(cols, col_rows, groups):
            for part, at, size in zip(pieces, starts(chunks), chunks):
                fold = fold + tile(rows, down, part, lab, sums, met, at, size, width)
        sums[line : line + 1, first : first + n] = sums[line : line + 1, first : first + n] + to_lanes(fold)


def far(new, ks, new_row, groups, sums, chunks, line):
    width, count = new[0].shape[1], sum(chunks)
    pairs = sum(chunks[k] for k in ks) * count * len(groups)
    cols = [piece for pieces, _, _ in groups for piece in pieces]
    return pl.pallas_call(
        functools.partial(
            far_kernel, width=width, chunks=tuple(chunks), news=len(new), ks=tuple(ks), groups=tuple(g[2] for g in groups), line=line
        ),
        out_shape=jax.ShapeDtypeStruct(sums.shape, jnp.float32),
        in_specs=[VMEM] * (len(new) + len(cols) + len(groups) + 2),
        out_specs=VMEM,
        compiler_params=PARAMS,
        cost_estimate=pl.CostEstimate(
            flops=2 * pairs * width, bytes_accessed=2 * width * count * (1 + len(groups)), transcendentals=pairs
        ),
    )(*new, *cols, new_row, *(g[1] for g in groups), sums)


def cut(count):
    tiles = count // LANES - 1
    return [tiles // 2 * LANES, (tiles - tiles // 2) * LANES, LANES]


def per_device(embeddings, labels):
    count, _ = embeddings.shape
    blk, sub = lax.axis_index("blk"), lax.axis_index("sub")
    chunks = cut(count)
    one = sub == 1
    low, high = blk & 1, (blk >> 1) & 1
    swapped, late = jnp.where(one, low, high) == 1, sub != high
    embeddings, labels, swapped, late, one, nil = lax.optimization_barrier((embeddings, labels, swapped, late, one, sub == 0))
    spans = list(zip(starts(chunks), chunks))
    first, second, cross = [], [], []
    own = [lax.slice_in_dim(embeddings, 0, chunks[0], axis=0)]
    first.append(exchange_mixed(own[0]))
    lab = labels[None, :]
    lab_other = exchange(lab, 1)
    lab_s = jnp.concatenate([lab, lab_other], axis=0)
    lab_x = exchange(lab_s, 2)
    lab_z = exchange(lab_s, 4)
    lab_d = exchange(lab_x, 4)
    source, _ = lax.optimization_barrier((embeddings, own[0]))
    own = own + list(split(source, spans[1:]))
    for k in range(1, len(chunks)):
        first.append(exchange_mixed(own[k]))
    partner = exchange(source, 1)
    other = split(partner, spans)
    for k in range(len(chunks)):
        second.append(exchange_mixed(other[k]))
    for k in range(len(chunks)):
        cross.append(exchange(first[k], 1))
    lab_all = jnp.concatenate([lab_s, lab_x, lab_z, lab_d], axis=0)
    first_lab, second_lab = jnp.where(one, lab_x[0:1], lab_z[0:1]), jnp.where(one, lab_x[1:2], lab_z[1:2])
    cross_lab = jnp.where(one, lab_z[1:2], lab_x[1:2])
    nobody = jnp.full_like(lab, -1)
    met_first = [jnp.where(swapped, b, a) for a, b in zip(own, other)]
    met_second = [jnp.where(swapped, a, b) for a, b in zip(own, other)]
    met_first_lab, met_second_lab = jnp.where(swapped, lab_other, lab), jnp.where(swapped, lab, lab_other)
    sums = near(own, other, lab, lab_other, chunks)
    for k in range(len(chunks)):
        sums = far(first[k : k + 1], [k], first_lab, [(met_first, met_first_lab, MET_FIRST)], sums, chunks, FIRST)
    early = [(cross, jnp.where(late, nobody, cross_lab), CROSS)]
    sums = far(first, range(len(chunks)), first_lab, early, sums, chunks, FIRST)
    meets = [(met_second, met_second_lab, MET_SECOND), (cross, jnp.where(late, cross_lab, nobody), CROSS)]
    for k in range(len(chunks)):
        sums = far(second[k : k + 1], [k], second_lab, meets, sums, chunks, SECOND)
    own_sum, met_a, met_b = sums[0:1], sums[1:2], sums[2:3]
    sums = jnp.concatenate(
        [own_sum + jnp.where(swapped, met_b, met_a), jnp.where(swapped, met_a, met_b), sums[3:6]], axis=0
    )
    part = spread(sums, one) + turned(spread(exchange(sums, 1), nil), 1)
    met = exchange(part[0:6], 3)
    part = part + turned(jnp.concatenate([met, jnp.zeros((2, count), jnp.float32)], axis=0), 3)
    part = part + turned(exchange(part, 5), 5)
    weight = 1.0 / part
    ident = jnp.arange(CLUSTERS, dtype=jnp.int32)
    mass = jnp.sum(jnp.where(lab_all[:, None, :] == ident[None, :, None], weight[:, None, :], 0.0), axis=(0, 2))
    bit = 8
    while bit < lax.axis_size("blk") * 2:
        mass = mass + exchange(mass, bit + 1)
        bit *= 2
    return weight[0], mass


def turned(rows, xor):
    return jnp.concatenate([rows[r ^ xor : (r ^ xor) + 1] for r in range(8)], axis=0)


def spread(sums, one):
    own, other, first, second, cross = (sums[r : r + 1] for r in range(5))
    zero = jnp.zeros_like(own)
    return jnp.concatenate(
        [
            own,
            other,
            jnp.where(one, first, zero),
            jnp.where(one, second, cross),
            jnp.where(one, zero, first),
            jnp.where(one, cross, second),
            zero,
            zero,
        ],
        axis=0,
    )


def solution(mesh):
    in_specs = (P(("parts", "blk", "sub"), None), P(("parts", "blk", "sub")))
    out_specs = (P(("parts", "blk", "sub")), P("parts"))
    return jax.shard_map(per_device, mesh=mesh, in_specs=in_specs, out_specs=out_specs, check_vma=False)
```

time: 65.1 us -> 66.3 us (1.018)
  waiting for transfers between devices: 26.8 us -> 24.7 us
  other arithmetic: 1.02 us -> 2.27 us
  local copies, waits for them, and re-layouts: 2.97 us -> 4.06 us
    pallas_call x5 -> x7, Pallas kernels: 7.27 us -> 9.4 us  [far(): pl.pallas_call(functools.partial(far_kernel, width=width, chunks=tuple(ch...]
    pallas_call x1, Pallas kernels: 5.6 us -> 3.91 us  [near(): pl.pallas_call(functools.partial(near_kernel, width=width, chunks=tuple(c...]
    ppermute x8 -> x6, waiting for transfers between devices: 7.87 us -> 6.49 us  [exchange_mixed(): lax.ppermute(value, AXES, [(i, i ^ 2 if i & 1 else i ^ 4) for i in range(...]
    select_n x5 -> x8, other arithmetic: 0.05 us -> 1.32 us  [the longest x3 1.26 us: per_device(): met_first = [jnp.where(swapped, b, a) for a, b in zip(own, other)]]
    slice x1 -> x2, local copies, waits for them, and re-layouts: 0.01 us -> 1.08 us  [the longest x1 1.08 us: per_device(): own = [lax.slice_in_dim(embeddings, 0, chunks[0], axis=0)]]
    ppermute x9 -> x12, waiting for transfers between devices: 19 us -> 18.3 us  [exchange(): return lax.ppermute(value, AXES, [(i, i ^ xor) for i in range(count)])]
    ppermute x9 -> x12, starting transfers between devices: 10.7 us -> 11.4 us  [exchange(): return lax.ppermute(value, AXES, [(i, i ^ xor) for i in range(count)])]
    ppermute x8 -> x6, starting transfers between devices: 9.48 us -> 9.19 us  [exchange_mixed(): lax.ppermute(value, AXES, [(i, i ^ 2 if i & 1 else i ^ 4) for i in range(...]
  transfers between devices with their start and end apart: 17 -> 18, of which waited for: 9 -> 8; matrix products, arithmetic and copies ran while one was open for 1% -> 4% of each run, Pallas kernels for 18% -> 19%
where the time goes in v2:
time: 66.3 us; the launch traced here: 66.1 us
  waiting for transfers between devices  24.7 us (37%)
  starting transfers between devices  20.6 us (31%)
  Pallas kernels  13.5 us (20%)
  local copies, waits for them, and re-layouts  4.06 us (6%)
  other arithmetic  2.27 us (3%)
  between operations  0.84 us (1%)
    ppermute x12, waiting for transfers between devices, exchange(): return lax.ppermute(value, AXES, [(i, i ^ xor) for i in range(count)])  18.3 us
    ppermute x12, starting transfers between devices, exchange(): return lax.ppermute(value, AXES, [(i, i ^ xor) for i in range(count)])  11.4 us
    pallas_call x7, Pallas kernels, far(): pl.pallas_call(functools.partial(far_kernel, width=width, chunks=tuple(ch...  9.4 us
    ppermute x6, starting transfers between devices, exchange_mixed(): lax.ppermute(value, AXES, [(i, i ^ 2 if i & 1 else i ^ 4) for i in range(...  9.19 us
    ppermute x6, waiting for transfers between devices, exchange_mixed(): lax.ppermute(value, AXES, [(i, i ^ 2 if i & 1 else i ^ 4) for i in range(...  6.49 us
    pallas_call x1, Pallas kernels, near(): pl.pallas_call(functools.partial(near_kernel, width=width, chunks=tuple(c...  3.91 us
    unnamed x4, local copies, waits for them, and re-layouts  1.41 us
  transfers between devices with their start and end apart: 18, of which 8 were waited for; matrix products, arithmetic and copies ran while one was open for 4% of the time, Pallas kernels for 19%

profile of v2, /device:TPU:0, one launch (start us, length us, event | category | flops | bytes accessed | tf_op | source)
XLA Modules:
  0.0 66.1 jit_solution(16367503685838715421)
XLA Ops:
  0.7 1.1 %slice.104.refs_0_ = bf16[256,1024]{1,0:T(8,128)(2,1)S(1)} slice(bf16[768,1024]{1,0:T(8,128)(2,1)} %source), slice={[0:256], [0:1024]} | slice | bytes 1048576 | tf_op jit(solution)/shard_map/slice | solution.py:168
  1.7 0.6 collective-permute-start
  2.3 0.7 %broadcast_in_dim.21.refs_6_ = s32[1,768]{1,0:T(1,128)S(1)} reshape(s32[768]{0:T(1024)} %param.3) | data formatting | bytes 6144 | tf_op jit(solution)/shard_map/broadcast_in_dim | solution.py:170
  3.0 1.4 %copy-done = bf16[768,1024]{1,0:T(8,128)(2,1)S(1)} copy-done((bf16[768,1024]{1,0:T(8,128)(2,1)S(1)}, bf16[768,1024]{1,0:T(8,128)(2,1)}, u32[]{:S(2)}) %copy-start) | copy-done | bytes 1572888
  4.5 3.1 %collective-permute-start.4 = (bf16[384,1024]{1,0:T(8,128)(2,1)S(1)}, bf16[384,1024]{1,0:T(8,128)(2,1)S(1)}, u32[]{:S(2)}, u32[]{:S(2)}) collective-permute-start(bf16[384,1024]{1,0:T(8,128)(2,1)S(1)} %get-tuple-element.19.refs_1_), channel_id=1, source_target_pairs={{0,4},{1,3},{2,6},{3,1},{4,0},{5,7},{6,2},{7,5},{8,12},{9,11},{10,... | collective-permute-start | bytes 2359304 | tf_op jit(solution)/shard_map/ppermute | solution.py:28
  7.7 1.9 %collective-permute-start.9 = (s32[2,768]{1,0:T(2,128)S(1)}, s32[2,768]{1,0:T(2,128)S(1)}, u32[]{:S(2)}, u32[]{:S(2)}) collective-permute-start(s32[2,768]{1,0:T(2,128)S(1)} %pad_add_fusion), channel_id=1, source_target_pairs={{0,2},{1,3},{2,0},{3,1},{4,6},{5,7},{6,4},{7,5},{8,10},{9,11},{10,... | collective-permute-start | bytes 18440 | tf_op jit(solution)/shard_map/ppermute | solution.py:23
  9.7 1.6 %collective-permute-start.10 = (s32[2,768]{1,0:T(2,128)S(1)}, s32[2,768]{1,0:T(2,128)S(1)}, u32[]{:S(2)}, u32[]{:S(2)}) collective-permute-start(s32[2,768]{1,0:T(2,128)S(1)} %pad_add_fusion), channel_id=1, source_target_pairs={{0,4},{1,5},{2,6},{3,7},{4,0},{5,1},{6,2},{7,3},{8,12},{9,13},{10,... | collective-permute-start | bytes 18440 | tf_op jit(solution)/shard_map/ppermute | solution.py:23
  11.5 1.9 %collective-permute-start.6 = (bf16[128,1024]{1,0:T(8,128)(2,1)S(1)}, bf16[128,1024]{1,0:T(8,128)(2,1)S(1)}, u32[]{:S(2)}, u32[]{:S(2)}) collective-permute-start(bf16[128,1024]{1,0:T(8,128)(2,1)S(1)} %get-tuple-element.21.refs_2_), channel_id=1, source_target_pairs={{0,4},{1,3},{2,6},{3,1},{4,0},{5,7},{6,2},{7,5},{8,12},{9,11},{10,... | collective-permute-start | bytes 786440 | tf_op jit(solution)/shard_map/ppermute | solution.py:28
  13.4 9.9 %collective-permute-done.10 = s32[2,768]{1,0:T(2,128)S(1)} collective-permute-done((s32[2,768]{1,0:T(2,128)S(1)}, s32[2,768]{1,0:T(2,128)S(1)}, u32[]{:S(2)}, u32[]{:S(2)}) %collective-permute-start.10) | collective-permute-done | bytes 6176 | tf_op jit(solution)/shard_map/ppermute | solution.py:23
  23.4 2.8 %collective-permute-done.6.refs_0_.refs_2_ = bf16[128,1024]{1,0:T(8,128)(2,1)S(1)} collective-permute-done((bf16[128,1024]{1,0:T(8,128)(2,1)S(1)}, bf16[128,1024]{1,0:T(8,128)(2,1)S(1)}, u32[]{:S(2)}, u32[]{:S(2)}) %collective-permute-start.6) | collective-permute-done | bytes 262176 | tf_op jit(solution)/shard_map/ppermute | solution.py:28
  26.2 1.8 %collective-permute-start.7 = (bf16[128,1024]{1,0:T(8,128)(2,1)S(1)}, bf16[128,1024]{1,0:T(8,128)(2,1)S(1)}, u32[]{:S(2)}, u32[]{:S(2)}) collective-permute-start(bf16[128,1024]{1,0:T(8,128)(2,1)S(1)} %collective-permute-done.6.refs_0_.refs_2_), channel_id=1, source_target_pairs={{0,1},{1,0},{2,3},{3,2},{4,5},{5,4},{6,7},{7,6},{8,9},{9,8},{10,11... | collective-permute-start | bytes 786440 | tf_op jit(solution)/shard_map/ppermute | solution.py:23
  28.7 1.9 %collective-permute-start.11 = (bf16[384,1024]{1,0:T(8,128)(2,1)S(1)}, bf16[384,1024]{1,0:T(8,128)(2,1)S(1)}, u32[]{:S(2)}, u32[]{:S(2)}) collective-permute-start(bf16[384,1024]{1,0:T(8,128)(2,1)S(1)} %get-tuple-element.20.refs_4_), channel_id=1, source_target_pairs={{0,4},{1,3},{2,6},{3,1},{4,0},{5,7},{6,2},{7,5},{8,12},{9,11},{10,... | collective-permute-start | bytes 2359304 | tf_op jit(solution)/shard_map/ppermute | solution.py:28
  30.6 1.1 %broadcast_select_fusion.2 = (bf16[256,1024]{1,0:T(8,128)(2,1)S(1)}, bf16[256,1024]{1,0:T(8,128)(2,1)S(1)}) fusion(bf16[256,1024]{1,0:T(8,128)(2,1)S(1)} %get-tuple-element.18.refs_3_, pred[]{:T(512)S(6)} %eq.23, bf16[768,1024]{1,0:T(8,128)(2,1)} %source), kind=kLoop, calls=%fused_computation.4 | loop fusion | flops 524288 | bytes 2097153 | tf_op jit(solution)/shard_map/jit(_where)/select_n | solution.py:190
  32.0 3.9 %shard_map.43.refs_6_ = f32[6,768]{1,0:T(8,128)S(1)} custom-call(bf16[256,1024]{1,0:T(8,128)(2,1)S(1)} %slice.104.refs_0_, bf16[384,1024]{1,0:T(8,128)(2,1)S(1)} %get-tuple-element.19.refs_1_, bf16[128,1024]{1,0:T(8,128)(2,1)S(1)} %get-tuple-element.21.refs_2_, bf16[256,1024]{1,0:T(8,128)(2,1)S(1)} %get-tuple-element.18.refs_3_, ...), custom_call_target="tpu_custom_call" | custom-call | flops 2415919104 | bytes 3145728 | tf_op jit(solution)/shard_map/pallas_call | solution.py:103
  35.9 0.9 %shard_map.44.refs_6_ = f32[6,768]{1,0:T(8,128)S(1)} custom-call(bf16[256,1024]{1,0:T(8,128)(2,1)S(1)} %collective-permute-done.2.refs_0_, bf16[256,1024]{1,0:T(8,128)(2,1)S(1)} %get-tuple-element.28.refs_1_, bf16[384,1024]{1,0:T(8,128)(2,1)S(1)} %get-tuple-element.30.refs_2_, bf16[128,1024]{1,0:T(8,128)(2,1)S(1)} %get-tuple-element.32.refs_3_, ...), custom_call_target="tpu_custom_call" | custom-call | flops 402653184 | bytes 3145728 | tf_op jit(solution)/shard_map/pallas_call | solution.py:139
  36.8 1.1 %shard_map.45.refs_6_ = f32[6,768]{1,0:T(8,128)S(1)} custom-call(bf16[384,1024]{1,0:T(8,128)(2,1)S(1)} %collective-permute-done.4.refs_0_.refs_1_, bf16[256,1024]{1,0:T(8,128)(2,1)S(1)} %get-tuple-element.28.refs_1_, bf16[384,1024]{1,0:T(8,128)(2,1)S(1)} %get-tuple-element.30.refs_2_, bf16[128,1024]{1,0:T(8,128)(2,1)S(1)} %get-tuple-element.32.refs_3_, ...), custom_call_target="tpu_custom_call" | custom-call | flops 603979776 | bytes 3145728 | tf_op jit(solution)/shard_map/pallas_call | solution.py:139
  37.9 0.7 %shard_map.46.refs_8_ = f32[6,768]{1,0:T(8,128)S(1)} custom-call(bf16[128,1024]{1,0:T(8,128)(2,1)S(1)} %collective-permute-done.6.refs_0_.refs_2_, bf16[256,1024]{1,0:T(8,128)(2,1)S(1)} %get-tuple-element.28.refs_1_, bf16[384,1024]{1,0:T(8,128)(2,1)S(1)} %get-tuple-element.30.refs_2_, bf16[128,1024]{1,0:T(8,128)(2,1)S(1)} %get-tuple-element.32.refs_3_, ...), custom_call_target="tpu_custom_call" | custom-call | flops 201326592 | bytes 3145728 | tf_op jit(solution)/shard_map/pallas_call | solution.py:139
  38.7 1.9 %collective-permute-start.1 = (bf16[128,1024]{1,0:T(8,128)(2,1)S(1)}, bf16[128,1024]{1,0:T(8,128)(2,1)S(1)}, u32[]{:S(2)}, u32[]{:S(2)}) collective-permute-start(bf16[128,1024]{1,0:T(8,128)(2,1)S(1)} %get-tuple-element.16.refs_5_), channel_id=1, source_target_pairs={{0,4},{1,3},{2,6},{3,1},{4,0},{5,7},{6,2},{7,5},{8,12},{9,11},{10,... | collective-permute-start | bytes 786440 | tf_op jit(solution)/shard_map/ppermute | solution.py:28
  40.6 2.1 %shard_map.47.refs_10_ = f32[6,768]{1,0:T(8,128)S(1)} custom-call(bf16[256,1024]{1,0:T(8,128)(2,1)S(1)} %collective-permute-done.2.refs_0_, bf16[384,1024]{1,0:T(8,128)(2,1)S(1)} %collective-permute-done.4.refs_0_.refs_1_, bf16[128,1024]{1,0:T(8,128)(2,1)S(1)} %collective-permute-done.6.refs_0_.refs_2_, ...), custom_call_target="tpu_custom_call" | custom-call | flops 1207959552 | bytes 3145728 | tf_op jit(solution)/shard_map/pallas_call | solution.py:139
  42.7 3.7 %collective-permute-done.12.refs_0_ = bf16[256,1024]{1,0:T(8,128)(2,1)S(1)} collective-permute-done((bf16[256,1024]{1,0:T(8,128)(2,1)S(1)}, bf16[256,1024]{1,0:T(8,128)(2,1)S(1)}, u32[]{:S(2)}, u32[]{:S(2)}) %collective-permute-start.12) | collective-permute-done | bytes 524320 | tf_op jit(solution)/shard_map/ppermute | solution.py:28
  46.4 1.4 %shard_map.48.refs_10_ = f32[6,768]{1,0:T(8,128)S(1)} custom-call(bf16[256,1024]{1,0:T(8,128)(2,1)S(1)} %collective-permute-done.12.refs_0_, bf16[256,1024]{1,0:T(8,128)(2,1)S(1)} %get-tuple-element.29.refs_1_, bf16[384,1024]{1,0:T(8,128)(2,1)S(1)} %get-tuple-element.31.refs_2_, bf16[128,1024]{1,0:T(8,128)(2,1)S(1)} %get-tuple-element.33.refs_3_, ...), custom_call_target="tpu_custom_call" | custom-call | flops 805306368 | bytes 4718592 | tf_op jit(solution)/shard_map/pallas_call | solution.py:139
  47.8 2.0 %shard_map.49.refs_10_ = f32[6,768]{1,0:T(8,128)S(1)} custom-call(bf16[384,1024]{1,0:T(8,128)(2,1)S(1)} %collective-permute-done.11.refs_0_, bf16[256,1024]{1,0:T(8,128)(2,1)S(1)} %get-tuple-element.29.refs_1_, bf16[384,1024]{1,0:T(8,128)(2,1)S(1)} %get-tuple-element.31.refs_2_, bf16[128,1024]{1,0:T(8,128)(2,1)S(1)} %get-tuple-element.33.refs_3_, ...), custom_call_target="tpu_custom_call" | custom-call | flops 1207959552 | bytes 4718592 | tf_op jit(solution)/shard_map/pallas_call | solution.py:139
  49.8 1.2 %shard_map.50 = f32[6,768]{1,0:T(8,128)S(1)} custom-call(bf16[128,1024]{1,0:T(8,128)(2,1)S(1)} %collective-permute-done.1.refs_0_, bf16[256,1024]{1,0:T(8,128)(2,1)S(1)} %get-tuple-element.29.refs_1_, bf16[384,1024]{1,0:T(8,128)(2,1)S(1)} %get-tuple-element.31.refs_2_, bf16[128,1024]{1,0:T(8,128)(2,1)S(1)} %get-tuple-element.33.refs_3_, ...), custom_call_target="tpu_custom_call" | custom-call | flops 402653184 | bytes 4718592 | tf_op jit(solution)/shard_map/pallas_call | solution.py:139
  51.2 1.1 %collective-permute-done.13 = f32[5,768]{1,0:T(8,128)S(1)} collective-permute-done((f32[5,768]{1,0:T(8,128)S(1)}, f32[5,768]{1,0:T(8,128)S(1)}, u32[]{:S(2)}, u32[]{:S(2)}) %collective-permute-start.13) | collective-permute-done | bytes 15392 | tf_op jit(solution)/shard_map/ppermute | solution.py:23
  52.4 1.6 %collective-permute-start.14 = (f32[6,768]{1,0:T(8,128)S(1)}, f32[6,768]{1,0:T(8,128)S(1)}, u32[]{:S(2)}, u32[]{:S(2)}) collective-permute-start(f32[6,768]{1,0:T(8,128)S(1)} %bitcast.1), channel_id=1, source_target_pairs={{0,3},{1,2},{2,1},{3,0},{4,7},{5,6},{6,5},{7,4},{8,11},{9,10},{10,... | collective-permute-start | bytes 55304 | tf_op jit(solution)/shard_map/ppermute | solution.py:23
  54.0 1.7 %collective-permute-done.14 = f32[6,768]{1,0:T(8,128)S(1)} collective-permute-done((f32[6,768]{1,0:T(8,128)S(1)}, f32[6,768]{1,0:T(8,128)S(1)}, u32[]{:S(2)}, u32[]{:S(2)}) %collective-permute-start.14) | collective-permute-done | bytes 18464 | tf_op jit(solution)/shard_map/ppermute | solution.py:23
  55.8 1.7 %collective-permute-start.15 = (f32[8,768]{1,0:T(8,128)S(1)}, f32[8,768]{1,0:T(8,128)S(1)}, u32[]{:S(2)}, u32[]{:S(2)}) collective-permute-start(f32[8,768]{1,0:T(8,128)S(1)} %add.29), channel_id=1, source_target_pairs={{0,5},{1,4},{2,7},{3,6},{4,1},{5,0},{6,3},{7,2},{8,13},{9,12},{10,... | collective-permute-start | bytes 73736 | tf_op jit(solution)/shard_map/ppermute | solution.py:23
  57.8 3.3 %collective-permute-done.16 = s32[2,768]{1,0:T(2,128)S(1)} collective-permute-done((s32[2,768]{1,0:T(2,128)S(1)}, s32[2,768]{1,0:T(2,128)S(1)}, u32[]{:S(2)}, u32[]{:S(2)}) %collective-permute-start.16) | collective-permute-done | bytes 6176 | tf_op jit(solution)/shard_map/ppermute | solution.py:23
  61.6 1.4 %collective-permute-start.17 = (f32[128]{0:T(128)S(1)}, f32[128]{0:T(128)S(1)}, u32[]{:S(2)}, u32[]{:S(2)}) collective-permute-start(f32[128]{0:T(128)S(1)} %select_reduce_fusion), channel_id=1, source_target_pairs={{0,9},{1,8},{2,11},{3,10},{4,13},{5,12},{6,15},{7,14},{8,1},{9,0},... | collective-permute-start | bytes 1544 | tf_op jit(solution)/shard_map/ppermute | solution.py:23
  63.1 0.6 slice_reduce_fusion
  63.7 1.9 %collective-permute-done.17 = f32[128]{0:T(128)S(1)} collective-permute-done((f32[128]{0:T(128)S(1)}, f32[128]{0:T(128)S(1)}, u32[]{:S(2)}, u32[]{:S(2)}) %collective-permute-start.17) | collective-permute-done | bytes 544 | tf_op jit(solution)/shard_map/ppermute | solution.py:23
  65.6 0.5 add.31
  (45 shorter events, 2.7 us)
Async XLA Ops:
  0.6 10.6 %copy-start.1 = (s32[768]{0:T(1024)S(1)}, s32[768]{0:T(1024)}, u32[]{:S(2)}) copy-start(s32[768]{0:T(1024)} %param.3) | copy-start | bytes 9220
  1.7 26.7 %collective-permute-start = (bf16[768,1024]{1,0:T(8,128)(2,1)}, bf16[768,1024]{1,0:T(8,128)(2,1)S(1)}, u32[]{:S(2)}, u32[]{:S(2)}) collective-permute-start(bf16[768,1024]{1,0:T(8,128)(2,1)} %source), channel_id=1, source_target_pairs={{0,1},{1,0},{2,3},{3,2},{4,5},{5,4},{6,7},{7,6},{8,9},{9,8},{10,11... | collective-permute-start | bytes 4718600 | tf_op jit(solution)/shard_map/ppermute | solution.py:23
  3.0 4.7 %collective-permute-start.8 = (s32[1,768]{1,0:T(1,128)S(1)}, s32[1,768]{1,0:T(1,128)S(1)}, u32[]{:S(2)}, u32[]{:S(2)}) collective-permute-start(s32[1,768]{1,0:T(1,128)S(1)} %broadcast_in_dim.21.refs_6_), channel_id=1, source_target_pairs={{0,1},{1,0},{2,3},{3,2},{4,5},{5,4},{6,7},{7,6},{8,9},{9,8},{10,11... | collective-permute-start | bytes 9224 | tf_op jit(solution)/shard_map/ppermute | solution.py:23
  3.0 1.4 %copy-start = (bf16[768,1024]{1,0:T(8,128)(2,1)S(1)}, bf16[768,1024]{1,0:T(8,128)(2,1)}, u32[]{:S(2)}) copy-start(bf16[768,1024]{1,0:T(8,128)(2,1)} %source) | copy-start | bytes 4718596
  4.5 23.4 %collective-permute-start.4 = (bf16[384,1024]{1,0:T(8,128)(2,1)S(1)}, bf16[384,1024]{1,0:T(8,128)(2,1)S(1)}, u32[]{:S(2)}, u32[]{:S(2)}) collective-permute-start(bf16[384,1024]{1,0:T(8,128)(2,1)S(1)} %get-tuple-element.19.refs_1_), channel_id=1, source_target_pairs={{0,4},{1,3},{2,6},{3,1},{4,0},{5,7},{6,2},{7,5},{8,12},{9,11},{10,... | collective-permute-start | bytes 2359304 | tf_op jit(solution)/shard_map/ppermute | solution.py:28
  7.6 20.3 %collective-permute-start.2 = (bf16[256,1024]{1,0:T(8,128)(2,1)S(1)}, bf16[256,1024]{1,0:T(8,128)(2,1)S(1)}, u32[]{:S(2)}, u32[]{:S(2)}) collective-permute-start(bf16[256,1024]{1,0:T(8,128)(2,1)S(1)} %slice.104.refs_0_), channel_id=1, source_target_pairs={{0,4},{1,3},{2,6},{3,1},{4,0},{5,7},{6,2},{7,5},{8,12},{9,11},{10,... | collective-permute-start | bytes 1572872 | tf_op jit(solution)/shard_map/ppermute | solution.py:28
  7.7 3.8 %collective-permute-start.9 = (s32[2,768]{1,0:T(2,128)S(1)}, s32[2,768]{1,0:T(2,128)S(1)}, u32[]{:S(2)}, u32[]{:S(2)}) collective-permute-start(s32[2,768]{1,0:T(2,128)S(1)} %pad_add_fusion), channel_id=1, source_target_pairs={{0,2},{1,3},{2,0},{3,1},{4,6},{5,7},{6,4},{7,5},{8,10},{9,11},{10,... | collective-permute-start | bytes 18440 | tf_op jit(solution)/shard_map/ppermute | solution.py:23
  9.7 13.7 %collective-permute-start.10 = (s32[2,768]{1,0:T(2,128)S(1)}, s32[2,768]{1,0:T(2,128)S(1)}, u32[]{:S(2)}, u32[]{:S(2)}) collective-permute-start(s32[2,768]{1,0:T(2,128)S(1)} %pad_add_fusion), channel_id=1, source_target_pairs={{0,4},{1,5},{2,6},{3,7},{4,0},{5,1},{6,2},{7,3},{8,12},{9,13},{10,... | collective-permute-start | bytes 18440 | tf_op jit(solution)/shard_map/ppermute | solution.py:23
  11.5 14.7 %collective-permute-start.6 = (bf16[128,1024]{1,0:T(8,128)(2,1)S(1)}, bf16[128,1024]{1,0:T(8,128)(2,1)S(1)}, u32[]{:S(2)}, u32[]{:S(2)}) collective-permute-start(bf16[128,1024]{1,0:T(8,128)(2,1)S(1)} %get-tuple-element.21.refs_2_), channel_id=1, source_target_pairs={{0,4},{1,3},{2,6},{3,1},{4,0},{5,7},{6,2},{7,5},{8,12},{9,11},{10,... | collective-permute-start | bytes 786440 | tf_op jit(solution)/shard_map/ppermute | solution.py:28
  26.2 12.5 %collective-permute-start.7 = (bf16[128,1024]{1,0:T(8,128)(2,1)S(1)}, bf16[128,1024]{1,0:T(8,128)(2,1)S(1)}, u32[]{:S(2)}, u32[]{:S(2)}) collective-permute-start(bf16[128,1024]{1,0:T(8,128)(2,1)S(1)} %collective-permute-done.6.refs_0_.refs_2_), channel_id=1, source_target_pairs={{0,1},{1,0},{2,3},{3,2},{4,5},{5,4},{6,7},{7,6},{8,9},{9,8},{10,11... | collective-permute-start | bytes 786440 | tf_op jit(solution)/shard_map/ppermute | solution.py:23
  27.9 12.6 %collective-permute-start.3 = (bf16[256,1024]{1,0:T(8,128)(2,1)S(1)}, bf16[256,1024]{1,0:T(8,128)(2,1)S(1)}, u32[]{:S(2)}, u32[]{:S(2)}) collective-permute-start(bf16[256,1024]{1,0:T(8,128)(2,1)S(1)} %collective-permute-done.2.refs_0_), channel_id=1, source_target_pairs={{0,1},{1,0},{2,3},{3,2},{4,5},{5,4},{6,7},{7,6},{8,9},{9,8},{10,11... | collective-permute-start | bytes 1572872 | tf_op jit(solution)/shard_map/ppermute | solution.py:23
  27.9 12.6 %collective-permute-start.5 = (bf16[384,1024]{1,0:T(8,128)(2,1)S(1)}, bf16[384,1024]{1,0:T(8,128)(2,1)S(1)}, u32[]{:S(2)}, u32[]{:S(2)}) collective-permute-start(bf16[384,1024]{1,0:T(8,128)(2,1)S(1)} %collective-permute-done.4.refs_0_.refs_1_), channel_id=1, source_target_pairs={{0,1},{1,0},{2,3},{3,2},{4,5},{5,4},{6,7},{7,6},{8,9},{9,8},{10,11... | collective-permute-start | bytes 2359304 | tf_op jit(solution)/shard_map/ppermute | solution.py:23
  28.7 19.1 %collective-permute-start.11 = (bf16[384,1024]{1,0:T(8,128)(2,1)S(1)}, bf16[384,1024]{1,0:T(8,128)(2,1)S(1)}, u32[]{:S(2)}, u32[]{:S(2)}) collective-permute-start(bf16[384,1024]{1,0:T(8,128)(2,1)S(1)} %get-tuple-element.20.refs_4_), channel_id=1, source_target_pairs={{0,4},{1,3},{2,6},{3,1},{4,0},{5,7},{6,2},{7,5},{8,12},{9,11},{10,... | collective-permute-start | bytes 2359304 | tf_op jit(solution)/shard_map/ppermute | solution.py:28
  31.7 14.7 %collective-permute-start.12 = (bf16[256,1024]{1,0:T(8,128)(2,1)S(1)}, bf16[256,1024]{1,0:T(8,128)(2,1)S(1)}, u32[]{:S(2)}, u32[]{:S(2)}) collective-permute-start(bf16[256,1024]{1,0:T(8,128)(2,1)S(1)} %get-tuple-element.18.refs_3_), channel_id=1, source_target_pairs={{0,4},{1,3},{2,6},{3,1},{4,0},{5,7},{6,2},{7,5},{8,12},{9,11},{10,... | collective-permute-start | bytes 1572872 | tf_op jit(solution)/shard_map/ppermute | solution.py:28
  38.7 11.1 %collective-permute-start.1 = (bf16[128,1024]{1,0:T(8,128)(2,1)S(1)}, bf16[128,1024]{1,0:T(8,128)(2,1)S(1)}, u32[]{:S(2)}, u32[]{:S(2)}) collective-permute-start(bf16[128,1024]{1,0:T(8,128)(2,1)S(1)} %get-tuple-element.16.refs_5_), channel_id=1, source_target_pairs={{0,4},{1,3},{2,6},{3,1},{4,0},{5,7},{6,2},{7,5},{8,12},{9,11},{10,... | collective-permute-start | bytes 786440 | tf_op jit(solution)/shard_map/ppermute | solution.py:28
  51.0 1.3 %collective-permute-start.13 = (f32[5,768]{1,0:T(8,128)S(1)}, f32[5,768]{1,0:T(8,128)S(1)}, u32[]{:S(2)}, u32[]{:S(2)}) collective-permute-start(f32[5,768]{1,0:T(8,128)S(1)} %pad_maximum_fusion), channel_id=1, source_target_pairs={{0,1},{1,0},{2,3},{3,2},{4,5},{5,4},{6,7},{7,6},{8,9},{9,8},{10,11... | collective-permute-start | bytes 46088 | tf_op jit(solution)/shard_map/ppermute | solution.py:23
  52.4 3.3 %collective-permute-start.14 = (f32[6,768]{1,0:T(8,128)S(1)}, f32[6,768]{1,0:T(8,128)S(1)}, u32[]{:S(2)}, u32[]{:S(2)}) collective-permute-start(f32[6,768]{1,0:T(8,128)S(1)} %bitcast.1), channel_id=1, source_target_pairs={{0,3},{1,2},{2,1},{3,0},{4,7},{5,6},{6,5},{7,4},{8,11},{9,10},{10,... | collective-permute-start | bytes 55304 | tf_op jit(solution)/shard_map/ppermute | solution.py:23
  55.8 5.3 %collective-permute-start.15 = (f32[8,768]{1,0:T(8,128)S(1)}, f32[8,768]{1,0:T(8,128)S(1)}, u32[]{:S(2)}, u32[]{:S(2)}) collective-permute-start(f32[8,768]{1,0:T(8,128)S(1)} %add.29), channel_id=1, source_target_pairs={{0,5},{1,4},{2,7},{3,6},{4,1},{5,0},{6,3},{7,2},{8,13},{9,12},{10,... | collective-permute-start | bytes 73736 | tf_op jit(solution)/shard_map/ppermute | solution.py:23
  57.5 3.6 %collective-permute-start.16 = (s32[2,768]{1,0:T(2,128)S(1)}, s32[2,768]{1,0:T(2,128)S(1)}, u32[]{:S(2)}, u32[]{:S(2)}) collective-permute-start(s32[2,768]{1,0:T(2,128)S(1)} %collective-permute-done.9), channel_id=1, source_target_pairs={{0,4},{1,5},{2,6},{3,7},{4,0},{5,1},{6,2},{7,3},{8,12},{9,13},{10,... | collective-permute-start | bytes 18440 | tf_op jit(solution)/shard_map/ppermute | solution.py:23
  61.6 4.0 %collective-permute-start.17 = (f32[128]{0:T(128)S(1)}, f32[128]{0:T(128)S(1)}, u32[]{:S(2)}, u32[]{:S(2)}) collective-permute-start(f32[128]{0:T(128)S(1)} %select_reduce_fusion), channel_id=1, source_target_pairs={{0,9},{1,8},{2,11},{3,10},{4,13},{5,12},{6,15},{7,14},{8,1},{9,0},... | collective-permute-start | bytes 1544 | tf_op jit(solution)/shard_map/ppermute | solution.py:23

commit v3 on v2

--- a/solution.py
+++ b/solution.py
@@ -25,7 +25,7 @@
 
 def exchange_mixed(value):
     count = lax.axis_size("blk") * lax.axis_size("sub")
-    return lax.ppermute(value, AXES, [(i, i ^ 2 if i & 1 else i ^ 4) for i in range(count)])
+    return lax.ppermute(value, AXES, [(i, i ^ 3 if i & 1 else i ^ 5) for i in range(count)])
 
 
 def down_rows(lab, first, size):
@@ -161,7 +161,7 @@
     chunks = cut(count)
     one = sub == 1
     low, high = blk & 1, (blk >> 1) & 1
-    swapped, late = jnp.where(one, low, high) == 1, sub != high
+    swapped, late = jnp.where(one, high, low) == 0, sub == high
     embeddings, labels, swapped, late, one, nil = lax.optimization_barrier((embeddings, labels, swapped, late, one, sub == 0))
     spans = list(zip(starts(chunks), chunks))
     first, second, cross = [], [], []
@@ -184,8 +184,8 @@
     for k in range(len(chunks)):
         cross.append(exchange(first[k], 1))
     lab_all = jnp.concatenate([lab_s, lab_x, lab_z, lab_d], axis=0)
-    first_lab, second_lab = jnp.where(one, lab_x[0:1], lab_z[0:1]), jnp.where(one, lab_x[1:2], lab_z[1:2])
-    cross_lab = jnp.where(one, lab_z[1:2], lab_x[1:2])
+    first_lab, second_lab = jnp.where(one, lab_z[1:2], lab_x[1:2]), jnp.where(one, lab_z[0:1], lab_x[0:1])
+    cross_lab = jnp.where(one, lab_x[0:1], lab_z[0:1])
     nobody = jnp.full_like(lab, -1)
     met_first = [jnp.where(swapped, b, a) for a, b in zip(own, other)]
     met_second = [jnp.where(swapped, a, b) for a, b in zip(own, other)]
@@ -227,10 +227,10 @@
         [
             own,
             other,
+            jnp.where(one, cross, second),
+            jnp.where(one, zero, first),
+            jnp.where(one, second, cross),
             jnp.where(one, first, zero),
-            jnp.where(one, second, cross),
-            jnp.where(one, zero, first),
-            jnp.where(one, cross, second),
             zero,
             zero,
         ],

time: 66.3 us -> 66.8 us (level)
  starting transfers between devices: 20.6 us -> 28.1 us
  waiting for transfers between devices: 24.7 us -> 17.7 us
    ppermute x6, starting transfers between devices: 9.19 us -> 19.9 us  [exchange_mixed(): lax.ppermute(value, AXES, [(i, i ^ 3 if i & 1 else i ^ 5) for i in range(...]
    ppermute x12, waiting for transfers between devices: 18.3 us -> 10.4 us  [exchange(): return lax.ppermute(value, AXES, [(i, i ^ xor) for i in range(count)])]
    ppermute x12, starting transfers between devices: 11.4 us -> 8.19 us  [exchange(): return lax.ppermute(value, AXES, [(i, i ^ xor) for i in range(count)])]
    ppermute x6, waiting for transfers between devices: 6.49 us -> 7.33 us  [exchange_mixed(): lax.ppermute(value, AXES, [(i, i ^ 3 if i & 1 else i ^ 5) for i in range(...]
  transfers between devices with their start and end apart: 18 -> 18, of which waited for: 8 -> 7; matrix products, arithmetic and copies ran while one was open for 4% -> 4% of each run, Pallas kernels for 19% -> 19%
where the time goes in v3:
time: 66.8 us; the launch traced here: 66.6 us
  starting transfers between devices  28.1 us (42%)
  waiting for transfers between devices  17.7 us (26%)
  Pallas kernels  13.5 us (20%)
  local copies, waits for them, and re-layouts  4.06 us (6%)
  other arithmetic  2.27 us (3%)
  between operations  0.83 us (1%)
    ppermute x6, starting transfers between devices, exchange_mixed(): lax.ppermute(value, AXES, [(i, i ^ 3 if i & 1 else i ^ 5) for i in range(...  19.9 us
    ppermute x12, waiting for transfers between devices, exchange(): return lax.ppermute(value, AXES, [(i, i ^ xor) for i in range(count)])  10.4 us
    pallas_call x7, Pallas kernels, far(): pl.pallas_call(functools.partial(far_kernel, width=width, chunks=tuple(ch...  9.4 us
    ppermute x12, starting transfers between devices, exchange(): return lax.ppermute(value, AXES, [(i, i ^ xor) for i in range(count)])  8.19 us
    ppermute x6, waiting for transfers between devices, exchange_mixed(): lax.ppermute(value, AXES, [(i, i ^ 3 if i & 1 else i ^ 5) for i in range(...  7.33 us
    pallas_call x1, Pallas kernels, near(): pl.pallas_call(functools.partial(near_kernel, width=width, chunks=tuple(c...  3.91 us
    unnamed x4, local copies, waits for them, and re-layouts  1.41 us
  transfers between devices with their start and end apart: 18, of which 7 were waited for; matrix products, arithmetic and copies ran while one was open for 4% of the time, Pallas kernels for 19%

profile of v3, /device:TPU:0, one launch (start us, length us, event | category | flops | bytes accessed | tf_op | source)
XLA Modules:
  0.0 66.6 jit_solution(2544860314922328536)
XLA Ops:
  0.7 1.1 %slice.104.refs_0_ = bf16[256,1024]{1,0:T(8,128)(2,1)S(1)} slice(bf16[768,1024]{1,0:T(8,128)(2,1)} %source), slice={[0:256], [0:1024]} | slice | bytes 1048576 | tf_op jit(solution)/shard_map/slice | solution.py:168
  1.7 0.6 collective-permute-start
  2.3 0.7 %broadcast_in_dim.21.refs_6_ = s32[1,768]{1,0:T(1,128)S(1)} reshape(s32[768]{0:T(1024)} %param.3) | data formatting | bytes 6144 | tf_op jit(solution)/shard_map/broadcast_in_dim | solution.py:170
  3.0 1.4 %copy-done = bf16[768,1024]{1,0:T(8,128)(2,1)S(1)} copy-done((bf16[768,1024]{1,0:T(8,128)(2,1)S(1)}, bf16[768,1024]{1,0:T(8,128)(2,1)}, u32[]{:S(2)}) %copy-start) | copy-done | bytes 1572888
  4.5 2.7 %collective-permute-start.4 = (bf16[384,1024]{1,0:T(8,128)(2,1)S(1)}, bf16[384,1024]{1,0:T(8,128)(2,1)S(1)}, u32[]{:S(2)}, u32[]{:S(2)}) collective-permute-start(bf16[384,1024]{1,0:T(8,128)(2,1)S(1)} %get-tuple-element.19.refs_1_), channel_id=1, source_target_pairs={{0,5},{1,2},{2,7},{3,0},{4,1},{5,6},{6,3},{7,4},{8,13},{9,10},{10,... | collective-permute-start | bytes 2359304 | tf_op jit(solution)/shard_map/ppermute | solution.py:28
  7.2 1.6 %collective-permute-start.2 = (bf16[256,1024]{1,0:T(8,128)(2,1)S(1)}, bf16[256,1024]{1,0:T(8,128)(2,1)S(1)}, u32[]{:S(2)}, u32[]{:S(2)}) collective-permute-start(bf16[256,1024]{1,0:T(8,128)(2,1)S(1)} %slice.104.refs_0_), channel_id=1, source_target_pairs={{0,5},{1,2},{2,7},{3,0},{4,1},{5,6},{6,3},{7,4},{8,13},{9,10},{10,... | collective-permute-start | bytes 1572872 | tf_op jit(solution)/shard_map/ppermute | solution.py:28
  8.8 0.6 collective-permute-start.10
  9.4 0.6 collective-permute-start.9
  10.1 2.5 %collective-permute-done.10 = s32[2,768]{1,0:T(2,128)S(1)} collective-permute-done((s32[2,768]{1,0:T(2,128)S(1)}, s32[2,768]{1,0:T(2,128)S(1)}, u32[]{:S(2)}, u32[]{:S(2)}) %collective-permute-start.10) | collective-permute-done | bytes 6176 | tf_op jit(solution)/shard_map/ppermute | solution.py:23
  12.6 11.8 %collective-permute-start.6 = (bf16[128,1024]{1,0:T(8,128)(2,1)S(1)}, bf16[128,1024]{1,0:T(8,128)(2,1)S(1)}, u32[]{:S(2)}, u32[]{:S(2)}) collective-permute-start(bf16[128,1024]{1,0:T(8,128)(2,1)S(1)} %get-tuple-element.21.refs_2_), channel_id=1, source_target_pairs={{0,5},{1,2},{2,7},{3,0},{4,1},{5,6},{6,3},{7,4},{8,13},{9,10},{10,... | collective-permute-start | bytes 786440 | tf_op jit(solution)/shard_map/ppermute | solution.py:28
  24.5 3.9 %collective-permute-done.6.refs_0_.refs_2_ = bf16[128,1024]{1,0:T(8,128)(2,1)S(1)} collective-permute-done((bf16[128,1024]{1,0:T(8,128)(2,1)S(1)}, bf16[128,1024]{1,0:T(8,128)(2,1)S(1)}, u32[]{:S(2)}, u32[]{:S(2)}) %collective-permute-start.6) | collective-permute-done | bytes 262176 | tf_op jit(solution)/shard_map/ppermute | solution.py:28
  29.3 1.8 %collective-permute-start.11 = (bf16[384,1024]{1,0:T(8,128)(2,1)S(1)}, bf16[384,1024]{1,0:T(8,128)(2,1)S(1)}, u32[]{:S(2)}, u32[]{:S(2)}) collective-permute-start(bf16[384,1024]{1,0:T(8,128)(2,1)S(1)} %get-tuple-element.20.refs_4_), channel_id=1, source_target_pairs={{0,5},{1,2},{2,7},{3,0},{4,1},{5,6},{6,3},{7,4},{8,13},{9,10},{10,... | collective-permute-start | bytes 2359304 | tf_op jit(solution)/shard_map/ppermute | solution.py:28
  31.1 1.1 %broadcast_select_fusion.2 = (bf16[256,1024]{1,0:T(8,128)(2,1)S(1)}, bf16[256,1024]{1,0:T(8,128)(2,1)S(1)}) fusion(bf16[256,1024]{1,0:T(8,128)(2,1)S(1)} %get-tuple-element.18.refs_3_, pred[]{:T(512)S(6)} %eq.26, bf16[768,1024]{1,0:T(8,128)(2,1)} %source), kind=kLoop, calls=%fused_computation.4 | loop fusion | flops 524288 | bytes 2097153 | tf_op jit(solution)/shard_map/jit(_where)/select_n | solution.py:190
  32.3 1.6 %collective-permute-start.12 = (bf16[256,1024]{1,0:T(8,128)(2,1)S(1)}, bf16[256,1024]{1,0:T(8,128)(2,1)S(1)}, u32[]{:S(2)}, u32[]{:S(2)}) collective-permute-start(bf16[256,1024]{1,0:T(8,128)(2,1)S(1)} %get-tuple-element.18.refs_3_), channel_id=1, source_target_pairs={{0,5},{1,2},{2,7},{3,0},{4,1},{5,6},{6,3},{7,4},{8,13},{9,10},{10,... | collective-permute-start | bytes 1572872 | tf_op jit(solution)/shard_map/ppermute | solution.py:28
  33.9 3.9 %shard_map.43.refs_6_ = f32[6,768]{1,0:T(8,128)S(1)} custom-call(bf16[256,1024]{1,0:T(8,128)(2,1)S(1)} %slice.104.refs_0_, bf16[384,1024]{1,0:T(8,128)(2,1)S(1)} %get-tuple-element.19.refs_1_, bf16[128,1024]{1,0:T(8,128)(2,1)S(1)} %get-tuple-element.21.refs_2_, bf16[256,1024]{1,0:T(8,128)(2,1)S(1)} %get-tuple-element.18.refs_3_, ...), custom_call_target="tpu_custom_call" | custom-call | flops 2415919104 | bytes 3145728 | tf_op jit(solution)/shard_map/pallas_call | solution.py:103
  37.8 0.9 %shard_map.44.refs_6_ = f32[6,768]{1,0:T(8,128)S(1)} custom-call(bf16[256,1024]{1,0:T(8,128)(2,1)S(1)} %collective-permute-done.2.refs_0_, bf16[256,1024]{1,0:T(8,128)(2,1)S(1)} %get-tuple-element.28.refs_1_, bf16[384,1024]{1,0:T(8,128)(2,1)S(1)} %get-tuple-element.30.refs_2_, bf16[128,1024]{1,0:T(8,128)(2,1)S(1)} %get-tuple-element.32.refs_3_, ...), custom_call_target="tpu_custom_call" | custom-call | flops 402653184 | bytes 3145728 | tf_op jit(solution)/shard_map/pallas_call | solution.py:139
  38.7 1.1 %shard_map.45.refs_6_ = f32[6,768]{1,0:T(8,128)S(1)} custom-call(bf16[384,1024]{1,0:T(8,128)(2,1)S(1)} %collective-permute-done.4.refs_0_.refs_1_, bf16[256,1024]{1,0:T(8,128)(2,1)S(1)} %get-tuple-element.28.refs_1_, bf16[384,1024]{1,0:T(8,128)(2,1)S(1)} %get-tuple-element.30.refs_2_, bf16[128,1024]{1,0:T(8,128)(2,1)S(1)} %get-tuple-element.32.refs_3_, ...), custom_call_target="tpu_custom_call" | custom-call | flops 603979776 | bytes 3145728 | tf_op jit(solution)/shard_map/pallas_call | solution.py:139
  39.8 0.7 %shard_map.46.refs_8_ = f32[6,768]{1,0:T(8,128)S(1)} custom-call(bf16[128,1024]{1,0:T(8,128)(2,1)S(1)} %collective-permute-done.6.refs_0_.refs_2_, bf16[256,1024]{1,0:T(8,128)(2,1)S(1)} %get-tuple-element.28.refs_1_, bf16[384,1024]{1,0:T(8,128)(2,1)S(1)} %get-tuple-element.30.refs_2_, bf16[128,1024]{1,0:T(8,128)(2,1)S(1)} %get-tuple-element.32.refs_3_, ...), custom_call_target="tpu_custom_call" | custom-call | flops 201326592 | bytes 3145728 | tf_op jit(solution)/shard_map/pallas_call | solution.py:139
  40.9 2.1 %shard_map.47.refs_10_ = f32[6,768]{1,0:T(8,128)S(1)} custom-call(bf16[256,1024]{1,0:T(8,128)(2,1)S(1)} %collective-permute-done.2.refs_0_, bf16[384,1024]{1,0:T(8,128)(2,1)S(1)} %collective-permute-done.4.refs_0_.refs_1_, bf16[128,1024]{1,0:T(8,128)(2,1)S(1)} %collective-permute-done.6.refs_0_.refs_2_, ...), custom_call_target="tpu_custom_call" | custom-call | flops 1207959552 | bytes 3145728 | tf_op jit(solution)/shard_map/pallas_call | solution.py:139
  43.0 3.4 %collective-permute-done.12.refs_0_ = bf16[256,1024]{1,0:T(8,128)(2,1)S(1)} collective-permute-done((bf16[256,1024]{1,0:T(8,128)(2,1)S(1)}, bf16[256,1024]{1,0:T(8,128)(2,1)S(1)}, u32[]{:S(2)}, u32[]{:S(2)}) %collective-permute-start.12) | collective-permute-done | bytes 524320 | tf_op jit(solution)/shard_map/ppermute | solution.py:28
  46.4 1.4 %shard_map.48.refs_10_ = f32[6,768]{1,0:T(8,128)S(1)} custom-call(bf16[256,1024]{1,0:T(8,128)(2,1)S(1)} %collective-permute-done.12.refs_0_, bf16[256,1024]{1,0:T(8,128)(2,1)S(1)} %get-tuple-element.29.refs_1_, bf16[384,1024]{1,0:T(8,128)(2,1)S(1)} %get-tuple-element.31.refs_2_, bf16[128,1024]{1,0:T(8,128)(2,1)S(1)} %get-tuple-element.33.refs_3_, ...), custom_call_target="tpu_custom_call" | custom-call | flops 805306368 | bytes 4718592 | tf_op jit(solution)/shard_map/pallas_call | solution.py:139
  47.8 2.0 %shard_map.49.refs_10_ = f32[6,768]{1,0:T(8,128)S(1)} custom-call(bf16[384,1024]{1,0:T(8,128)(2,1)S(1)} %collective-permute-done.11.refs_0_, bf16[256,1024]{1,0:T(8,128)(2,1)S(1)} %get-tuple-element.29.refs_1_, bf16[384,1024]{1,0:T(8,128)(2,1)S(1)} %get-tuple-element.31.refs_2_, bf16[128,1024]{1,0:T(8,128)(2,1)S(1)} %get-tuple-element.33.refs_3_, ...), custom_call_target="tpu_custom_call" | custom-call | flops 1207959552 | bytes 4718592 | tf_op jit(solution)/shard_map/pallas_call | solution.py:139
  49.8 1.2 %shard_map.50 = f32[6,768]{1,0:T(8,128)S(1)} custom-call(bf16[128,1024]{1,0:T(8,128)(2,1)S(1)} %collective-permute-done.1.refs_0_, bf16[256,1024]{1,0:T(8,128)(2,1)S(1)} %get-tuple-element.29.refs_1_, bf16[384,1024]{1,0:T(8,128)(2,1)S(1)} %get-tuple-element.31.refs_2_, bf16[128,1024]{1,0:T(8,128)(2,1)S(1)} %get-tuple-element.33.refs_3_, ...), custom_call_target="tpu_custom_call" | custom-call | flops 402653184 | bytes 4718592 | tf_op jit(solution)/shard_map/pallas_call | solution.py:139
  51.1 0.8 %collective-permute-start.13 = (f32[5,768]{1,0:T(8,128)S(1)}, f32[5,768]{1,0:T(8,128)S(1)}, u32[]{:S(2)}, u32[]{:S(2)}) collective-permute-start(f32[5,768]{1,0:T(8,128)S(1)} %pad_maximum_fusion), channel_id=1, source_target_pairs={{0,1},{1,0},{2,3},{3,2},{4,5},{5,4},{6,7},{7,6},{8,9},{9,8},{10,11... | collective-permute-start | bytes 46088 | tf_op jit(solution)/shard_map/ppermute | solution.py:23
  51.9 0.8 %collective-permute-done.13 = f32[5,768]{1,0:T(8,128)S(1)} collective-permute-done((f32[5,768]{1,0:T(8,128)S(1)}, f32[5,768]{1,0:T(8,128)S(1)}, u32[]{:S(2)}, u32[]{:S(2)}) %collective-permute-start.13) | collective-permute-done | bytes 15392 | tf_op jit(solution)/shard_map/ppermute | solution.py:23
  52.8 1.6 %collective-permute-start.14 = (f32[6,768]{1,0:T(8,128)S(1)}, f32[6,768]{1,0:T(8,128)S(1)}, u32[]{:S(2)}, u32[]{:S(2)}) collective-permute-start(f32[6,768]{1,0:T(8,128)S(1)} %bitcast.1), channel_id=1, source_target_pairs={{0,3},{1,2},{2,1},{3,0},{4,7},{5,6},{6,5},{7,4},{8,11},{9,10},{10,... | collective-permute-start | bytes 55304 | tf_op jit(solution)/shard_map/ppermute | solution.py:23
  54.5 1.7 %collective-permute-done.14 = f32[6,768]{1,0:T(8,128)S(1)} collective-permute-done((f32[6,768]{1,0:T(8,128)S(1)}, f32[6,768]{1,0:T(8,128)S(1)}, u32[]{:S(2)}, u32[]{:S(2)}) %collective-permute-start.14) | collective-permute-done | bytes 18464 | tf_op jit(solution)/shard_map/ppermute | solution.py:23
  56.2 1.7 %collective-permute-start.15 = (f32[8,768]{1,0:T(8,128)S(1)}, f32[8,768]{1,0:T(8,128)S(1)}, u32[]{:S(2)}, u32[]{:S(2)}) collective-permute-start(f32[8,768]{1,0:T(8,128)S(1)} %add.29), channel_id=1, source_target_pairs={{0,5},{1,4},{2,7},{3,6},{4,1},{5,0},{6,3},{7,2},{8,13},{9,12},{10,... | collective-permute-start | bytes 73736 | tf_op jit(solution)/shard_map/ppermute | solution.py:23
  58.3 3.3 %collective-permute-done.16 = s32[2,768]{1,0:T(2,128)S(1)} collective-permute-done((s32[2,768]{1,0:T(2,128)S(1)}, s32[2,768]{1,0:T(2,128)S(1)}, u32[]{:S(2)}, u32[]{:S(2)}) %collective-permute-start.16) | collective-permute-done | bytes 6176 | tf_op jit(solution)/shard_map/ppermute | solution.py:23
  62.1 1.3 %collective-permute-start.17 = (f32[128]{0:T(128)S(1)}, f32[128]{0:T(128)S(1)}, u32[]{:S(2)}, u32[]{:S(2)}) collective-permute-start(f32[128]{0:T(128)S(1)} %select_reduce_fusion), channel_id=1, source_target_pairs={{0,9},{1,8},{2,11},{3,10},{4,13},{5,12},{6,15},{7,14},{8,1},{9,0},... | collective-permute-start | bytes 1544 | tf_op jit(solution)/shard_map/ppermute | solution.py:23
  63.4 0.6 slice_reduce_fusion
  64.0 2.1 %collective-permute-done.17 = f32[128]{0:T(128)S(1)} collective-permute-done((f32[128]{0:T(128)S(1)}, f32[128]{0:T(128)S(1)}, u32[]{:S(2)}, u32[]{:S(2)}) %collective-permute-start.17) | collective-permute-done | bytes 544 | tf_op jit(solution)/shard_map/ppermute | solution.py:23
  (45 shorter events, 3.0 us)
Async XLA Ops:
  0.6 9.4 %copy-start.1 = (s32[768]{0:T(1024)S(1)}, s32[768]{0:T(1024)}, u32[]{:S(2)}) copy-start(s32[768]{0:T(1024)} %param.3) | copy-start | bytes 9220
  1.7 27.3 %collective-permute-start = (bf16[768,1024]{1,0:T(8,128)(2,1)}, bf16[768,1024]{1,0:T(8,128)(2,1)S(1)}, u32[]{:S(2)}, u32[]{:S(2)}) collective-permute-start(bf16[768,1024]{1,0:T(8,128)(2,1)} %source), channel_id=1, source_target_pairs={{0,1},{1,0},{2,3},{3,2},{4,5},{5,4},{6,7},{7,6},{8,9},{9,8},{10,11... | collective-permute-start | bytes 4718600 | tf_op jit(solution)/shard_map/ppermute | solution.py:23
  3.0 5.8 %collective-permute-start.8 = (s32[1,768]{1,0:T(1,128)S(1)}, s32[1,768]{1,0:T(1,128)S(1)}, u32[]{:S(2)}, u32[]{:S(2)}) collective-permute-start(s32[1,768]{1,0:T(1,128)S(1)} %broadcast_in_dim.21.refs_6_), channel_id=1, source_target_pairs={{0,1},{1,0},{2,3},{3,2},{4,5},{5,4},{6,7},{7,6},{8,9},{9,8},{10,11... | collective-permute-start | bytes 9224 | tf_op jit(solution)/shard_map/ppermute | solution.py:23
  3.0 1.4 %copy-start = (bf16[768,1024]{1,0:T(8,128)(2,1)S(1)}, bf16[768,1024]{1,0:T(8,128)(2,1)}, u32[]{:S(2)}) copy-start(bf16[768,1024]{1,0:T(8,128)(2,1)} %source) | copy-start | bytes 4718596
  4.5 24.4 %collective-permute-start.4 = (bf16[384,1024]{1,0:T(8,128)(2,1)S(1)}, bf16[384,1024]{1,0:T(8,128)(2,1)S(1)}, u32[]{:S(2)}, u32[]{:S(2)}) collective-permute-start(bf16[384,1024]{1,0:T(8,128)(2,1)S(1)} %get-tuple-element.19.refs_1_), channel_id=1, source_target_pairs={{0,5},{1,2},{2,7},{3,0},{4,1},{5,6},{6,3},{7,4},{8,13},{9,10},{10,... | collective-permute-start | bytes 2359304 | tf_op jit(solution)/shard_map/ppermute | solution.py:28
  7.2 21.3 %collective-permute-start.2 = (bf16[256,1024]{1,0:T(8,128)(2,1)S(1)}, bf16[256,1024]{1,0:T(8,128)(2,1)S(1)}, u32[]{:S(2)}, u32[]{:S(2)}) collective-permute-start(bf16[256,1024]{1,0:T(8,128)(2,1)S(1)} %slice.104.refs_0_), channel_id=1, source_target_pairs={{0,5},{1,2},{2,7},{3,0},{4,1},{5,6},{6,3},{7,4},{8,13},{9,10},{10,... | collective-permute-start | bytes 1572872 | tf_op jit(solution)/shard_map/ppermute | solution.py:28
  8.8 3.8 %collective-permute-start.10 = (s32[2,768]{1,0:T(2,128)S(1)}, s32[2,768]{1,0:T(2,128)S(1)}, u32[]{:S(2)}, u32[]{:S(2)}) collective-permute-start(s32[2,768]{1,0:T(2,128)S(1)} %pad_add_fusion), channel_id=1, source_target_pairs={{0,2},{1,3},{2,0},{3,1},{4,6},{5,7},{6,4},{7,5},{8,10},{9,11},{10,... | collective-permute-start | bytes 18440 | tf_op jit(solution)/shard_map/ppermute | solution.py:23
  9.4 15.0 %collective-permute-start.9 = (s32[2,768]{1,0:T(2,128)S(1)}, s32[2,768]{1,0:T(2,128)S(1)}, u32[]{:S(2)}, u32[]{:S(2)}) collective-permute-start(s32[2,768]{1,0:T(2,128)S(1)} %pad_add_fusion), channel_id=1, source_target_pairs={{0,4},{1,5},{2,6},{3,7},{4,0},{5,1},{6,2},{7,3},{8,12},{9,13},{10,... | collective-permute-start | bytes 18440 | tf_op jit(solution)/shard_map/ppermute | solution.py:23
  12.6 15.8 %collective-permute-start.6 = (bf16[128,1024]{1,0:T(8,128)(2,1)S(1)}, bf16[128,1024]{1,0:T(8,128)(2,1)S(1)}, u32[]{:S(2)}, u32[]{:S(2)}) collective-permute-start(bf16[128,1024]{1,0:T(8,128)(2,1)S(1)} %get-tuple-element.21.refs_2_), channel_id=1, source_target_pairs={{0,5},{1,2},{2,7},{3,0},{4,1},{5,6},{6,3},{7,4},{8,13},{9,10},{10,... | collective-permute-start | bytes 786440 | tf_op jit(solution)/shard_map/ppermute | solution.py:28
  28.4 12.1 %collective-permute-start.7 = (bf16[128,1024]{1,0:T(8,128)(2,1)S(1)}, bf16[128,1024]{1,0:T(8,128)(2,1)S(1)}, u32[]{:S(2)}, u32[]{:S(2)}) collective-permute-start(bf16[128,1024]{1,0:T(8,128)(2,1)S(1)} %collective-permute-done.6.refs_0_.refs_2_), channel_id=1, source_target_pairs={{0,1},{1,0},{2,3},{3,2},{4,5},{5,4},{6,7},{7,6},{8,9},{9,8},{10,11... | collective-permute-start | bytes 786440 | tf_op jit(solution)/shard_map/ppermute | solution.py:23
  28.5 12.4 %collective-permute-start.3 = (bf16[256,1024]{1,0:T(8,128)(2,1)S(1)}, bf16[256,1024]{1,0:T(8,128)(2,1)S(1)}, u32[]{:S(2)}, u32[]{:S(2)}) collective-permute-start(bf16[256,1024]{1,0:T(8,128)(2,1)S(1)} %collective-permute-done.2.refs_0_), channel_id=1, source_target_pairs={{0,1},{1,0},{2,3},{3,2},{4,5},{5,4},{6,7},{7,6},{8,9},{9,8},{10,11... | collective-permute-start | bytes 1572872 | tf_op jit(solution)/shard_map/ppermute | solution.py:23
  28.9 12.0 %collective-permute-start.5 = (bf16[384,1024]{1,0:T(8,128)(2,1)S(1)}, bf16[384,1024]{1,0:T(8,128)(2,1)S(1)}, u32[]{:S(2)}, u32[]{:S(2)}) collective-permute-start(bf16[384,1024]{1,0:T(8,128)(2,1)S(1)} %collective-permute-done.4.refs_0_.refs_1_), channel_id=1, source_target_pairs={{0,1},{1,0},{2,3},{3,2},{4,5},{5,4},{6,7},{7,6},{8,9},{9,8},{10,11... | collective-permute-start | bytes 2359304 | tf_op jit(solution)/shard_map/ppermute | solution.py:23
  29.3 18.5 %collective-permute-start.11 = (bf16[384,1024]{1,0:T(8,128)(2,1)S(1)}, bf16[384,1024]{1,0:T(8,128)(2,1)S(1)}, u32[]{:S(2)}, u32[]{:S(2)}) collective-permute-start(bf16[384,1024]{1,0:T(8,128)(2,1)S(1)} %get-tuple-element.20.refs_4_), channel_id=1, source_target_pairs={{0,5},{1,2},{2,7},{3,0},{4,1},{5,6},{6,3},{7,4},{8,13},{9,10},{10,... | collective-permute-start | bytes 2359304 | tf_op jit(solution)/shard_map/ppermute | solution.py:28
  32.3 14.1 %collective-permute-start.12 = (bf16[256,1024]{1,0:T(8,128)(2,1)S(1)}, bf16[256,1024]{1,0:T(8,128)(2,1)S(1)}, u32[]{:S(2)}, u32[]{:S(2)}) collective-permute-start(bf16[256,1024]{1,0:T(8,128)(2,1)S(1)} %get-tuple-element.18.refs_3_), channel_id=1, source_target_pairs={{0,5},{1,2},{2,7},{3,0},{4,1},{5,6},{6,3},{7,4},{8,13},{9,10},{10,... | collective-permute-start | bytes 1572872 | tf_op jit(solution)/shard_map/ppermute | solution.py:28
  40.5 9.3 %collective-permute-start.1 = (bf16[128,1024]{1,0:T(8,128)(2,1)S(1)}, bf16[128,1024]{1,0:T(8,128)(2,1)S(1)}, u32[]{:S(2)}, u32[]{:S(2)}) collective-permute-start(bf16[128,1024]{1,0:T(8,128)(2,1)S(1)} %get-tuple-element.16.refs_5_), channel_id=1, source_target_pairs={{0,5},{1,2},{2,7},{3,0},{4,1},{5,6},{6,3},{7,4},{8,13},{9,10},{10,... | collective-permute-start | bytes 786440 | tf_op jit(solution)/shard_map/ppermute | solution.py:28
  51.1 1.7 %collective-permute-start.13 = (f32[5,768]{1,0:T(8,128)S(1)}, f32[5,768]{1,0:T(8,128)S(1)}, u32[]{:S(2)}, u32[]{:S(2)}) collective-permute-start(f32[5,768]{1,0:T(8,128)S(1)} %pad_maximum_fusion), channel_id=1, source_target_pairs={{0,1},{1,0},{2,3},{3,2},{4,5},{5,4},{6,7},{7,6},{8,9},{9,8},{10,11... | collective-permute-start | bytes 46088 | tf_op jit(solution)/shard_map/ppermute | solution.py:23
  52.8 3.3 %collective-permute-start.14 = (f32[6,768]{1,0:T(8,128)S(1)}, f32[6,768]{1,0:T(8,128)S(1)}, u32[]{:S(2)}, u32[]{:S(2)}) collective-permute-start(f32[6,768]{1,0:T(8,128)S(1)} %bitcast.1), channel_id=1, source_target_pairs={{0,3},{1,2},{2,1},{3,0},{4,7},{5,6},{6,5},{7,4},{8,11},{9,10},{10,... | collective-permute-start | bytes 55304 | tf_op jit(solution)/shard_map/ppermute | solution.py:23
  56.2 5.4 %collective-permute-start.15 = (f32[8,768]{1,0:T(8,128)S(1)}, f32[8,768]{1,0:T(8,128)S(1)}, u32[]{:S(2)}, u32[]{:S(2)}) collective-permute-start(f32[8,768]{1,0:T(8,128)S(1)} %add.29), channel_id=1, source_target_pairs={{0,5},{1,4},{2,7},{3,6},{4,1},{5,0},{6,3},{7,2},{8,13},{9,12},{10,... | collective-permute-start | bytes 73736 | tf_op jit(solution)/shard_map/ppermute | solution.py:23
  57.9 3.6 %collective-permute-start.16 = (s32[2,768]{1,0:T(2,128)S(1)}, s32[2,768]{1,0:T(2,128)S(1)}, u32[]{:S(2)}, u32[]{:S(2)}) collective-permute-start(s32[2,768]{1,0:T(2,128)S(1)} %collective-permute-done.10), channel_id=1, source_target_pairs={{0,4},{1,5},{2,6},{3,7},{4,0},{5,1},{6,2},{7,3},{8,12},{9,13},{10,... | collective-permute-start | bytes 18440 | tf_op jit(solution)/shard_map/ppermute | solution.py:23
  62.1 4.0 %collective-permute-start.17 = (f32[128]{0:T(128)S(1)}, f32[128]{0:T(128)S(1)}, u32[]{:S(2)}, u32[]{:S(2)}) collective-permute-start(f32[128]{0:T(128)S(1)} %select_reduce_fusion), channel_id=1, source_target_pairs={{0,9},{1,8},{2,11},{3,10},{4,13},{5,12},{6,15},{7,14},{8,1},{9,0},... | collective-permute-start | bytes 1544 | tf_op jit(solution)/shard_map/ppermute | solution.py:23

commit v4 on v3

--- a/solution.py
+++ b/solution.py
@@ -150,9 +150,12 @@
     )(*new, *cols, new_row, *(g[1] for g in groups), sums)
 
 
+CHUNKS = 3
+
+
 def cut(count):
-    tiles = count // LANES - 1
-    return [tiles // 2 * LANES, (tiles - tiles // 2) * LANES, LANES]
+    base, more = divmod(count // LANES, CHUNKS)
+    return [(base + (k < more)) * LANES for k in range(CHUNKS)]
 
 
 def per_device(embeddings, labels):
@@ -202,10 +205,9 @@
     sums = jnp.concatenate(
         [own_sum + jnp.where(swapped, met_b, met_a), jnp.where(swapped, met_a, met_b), sums[3:6]], axis=0
     )
-    part = spread(sums, one) + turned(spread(exchange(sums, 1), nil), 1)
-    met = exchange(part[0:6], 3)
-    part = part + turned(jnp.concatenate([met, jnp.zeros((2, count), jnp.float32)], axis=0), 3)
-    part = part + turned(exchange(part, 5), 5)
+    part = spread(sums, one) + turned(spread(exchange(sums, 5), nil), 5)
+    part = part + turned(exchange(part, 3), 3)
+    part = part + turned(exchange(part, 1), 1)
     weight = 1.0 / part
     ident = jnp.arange(CLUSTERS, dtype=jnp.int32)
     mass = jnp.sum(jnp.where(lab_all[:, None, :] == ident[None, :, None], weight[:, None, :], 0.0), axis=(0, 2))

time: 66.8 us -> 66.8 us (level)
  waiting for transfers between devices: 17.7 us -> 33.1 us
  starting transfers between devices: 28.1 us -> 15.3 us
  Pallas kernels: 13.5 us -> 10.9 us
    ppermute x12, waiting for transfers between devices: 10.4 us -> 26.5 us  [exchange(): return lax.ppermute(value, AXES, [(i, i ^ xor) for i in range(count)])]
    ppermute x6, starting transfers between devices: 19.9 us -> 4.36 us  [exchange_mixed(): lax.ppermute(value, AXES, [(i, i ^ 3 if i & 1 else i ^ 5) for i in range(...]
    ppermute x12, starting transfers between devices: 8.19 us -> 10.9 us  [exchange(): return lax.ppermute(value, AXES, [(i, i ^ xor) for i in range(count)])]
    pallas_call x7, Pallas kernels: 9.4 us -> 7.57 us  [far(): pl.pallas_call(functools.partial(far_kernel, width=width, chunks=tuple(ch...]
    pallas_call x1, Pallas kernels: 3.91 us -> 3.14 us  [near(): pl.pallas_call(functools.partial(near_kernel, width=width, chunks=tuple(c...]
  transfers between devices with their start and end apart: 18 -> 18, of which waited for: 7 -> 8; matrix products, arithmetic and copies ran while one was open for 4% -> 4% of each run, Pallas kernels for 19% -> 15%
where the time goes in v4:
time: 66.8 us; the launch traced here: 66.5 us
  waiting for transfers between devices  33.1 us (50%)
  starting transfers between devices  15.3 us (23%)
  Pallas kernels  10.9 us (16%)
  local copies, waits for them, and re-layouts  4.07 us (6%)
  other arithmetic  2.27 us (3%)
  between operations  0.86 us (1%)
    ppermute x12, waiting for transfers between devices, exchange(): return lax.ppermute(value, AXES, [(i, i ^ xor) for i in range(count)])  26.5 us
    ppermute x12, starting transfers between devices, exchange(): return lax.ppermute(value, AXES, [(i, i ^ xor) for i in range(count)])  10.9 us
    pallas_call x7, Pallas kernels, far(): pl.pallas_call(functools.partial(far_kernel, width=width, chunks=tuple(ch...  7.57 us
    ppermute x6, waiting for transfers between devices, exchange_mixed(): lax.ppermute(value, AXES, [(i, i ^ 3 if i & 1 else i ^ 5) for i in range(...  6.67 us
    ppermute x6, starting transfers between devices, exchange_mixed(): lax.ppermute(value, AXES, [(i, i ^ 3 if i & 1 else i ^ 5) for i in range(...  4.36 us
    pallas_call x1, Pallas kernels, near(): pl.pallas_call(functools.partial(near_kernel, width=width, chunks=tuple(c...  3.14 us
    unnamed x4, local copies, waits for them, and re-layouts  1.41 us
  transfers between devices with their start and end apart: 18, of which 8 were waited for; matrix products, arithmetic and copies ran while one was open for 4% of the time, Pallas kernels for 15%

profile of v4, /device:TPU:0, one launch (start us, length us, event | category | flops | bytes accessed | tf_op | source)
XLA Modules:
  0.0 66.5 jit_solution(12123205751792081404)
XLA Ops:
  0.7 1.1 %slice.107.refs_0_ = bf16[256,1024]{1,0:T(8,128)(2,1)S(1)} slice(bf16[768,1024]{1,0:T(8,128)(2,1)} %source), slice={[0:256], [0:1024]} | slice | bytes 1048576 | tf_op jit(solution)/shard_map/slice | solution.py:171
  1.7 0.6 collective-permute-start
  2.3 0.7 %broadcast_in_dim.21.refs_6_ = s32[1,768]{1,0:T(1,128)S(1)} reshape(s32[768]{0:T(1024)} %param.3) | data formatting | bytes 6144 | tf_op jit(solution)/shard_map/broadcast_in_dim | solution.py:173
  3.0 2.5 %collective-permute-done.8.refs_7_ = s32[1,768]{1,0:T(1,128)S(1)} collective-permute-done((s32[1,768]{1,0:T(1,128)S(1)}, s32[1,768]{1,0:T(1,128)S(1)}, u32[]{:S(2)}, u32[]{:S(2)}) %collective-permute-start.8) | collective-permute-done | bytes 3104 | tf_op jit(solution)/shard_map/ppermute | solution.py:23
  5.6 2.9 %collective-permute-start.10 = (s32[2,768]{1,0:T(2,128)S(1)}, s32[2,768]{1,0:T(2,128)S(1)}, u32[]{:S(2)}, u32[]{:S(2)}) collective-permute-start(s32[2,768]{1,0:T(2,128)S(1)} %pad_add_fusion), channel_id=1, source_target_pairs={{0,2},{1,3},{2,0},{3,1},{4,6},{5,7},{6,4},{7,5},{8,10},{9,11},{10,... | collective-permute-start | bytes 18440 | tf_op jit(solution)/shard_map/ppermute | solution.py:23
  8.5 1.0 %collective-permute-start.2 = (bf16[256,1024]{1,0:T(8,128)(2,1)S(1)}, bf16[256,1024]{1,0:T(8,128)(2,1)S(1)}, u32[]{:S(2)}, u32[]{:S(2)}) collective-permute-start(bf16[256,1024]{1,0:T(8,128)(2,1)S(1)} %slice.107.refs_0_), channel_id=1, source_target_pairs={{0,5},{1,2},{2,7},{3,0},{4,1},{5,6},{6,3},{7,4},{8,13},{9,10},{10,... | collective-permute-start | bytes 1572872 | tf_op jit(solution)/shard_map/ppermute | solution.py:28
  9.5 1.4 %copy-done = bf16[768,1024]{1,0:T(8,128)(2,1)S(1)} copy-done((bf16[768,1024]{1,0:T(8,128)(2,1)S(1)}, bf16[768,1024]{1,0:T(8,128)(2,1)}, u32[]{:S(2)}) %copy-start) | copy-done | bytes 1572888
  11.0 0.8 %collective-permute-start.4 = (bf16[256,1024]{1,0:T(8,128)(2,1)S(1)}, bf16[256,1024]{1,0:T(8,128)(2,1)S(1)}, u32[]{:S(2)}, u32[]{:S(2)}) collective-permute-start(bf16[256,1024]{1,0:T(8,128)(2,1)S(1)} %get-tuple-element.19.refs_1_), channel_id=1, source_target_pairs={{0,5},{1,2},{2,7},{3,0},{4,1},{5,6},{6,3},{7,4},{8,13},{9,10},{10,... | collective-permute-start | bytes 1572872 | tf_op jit(solution)/shard_map/ppermute | solution.py:28
  11.9 1.4 %collective-permute-start.9 = (s32[2,768]{1,0:T(2,128)S(1)}, s32[2,768]{1,0:T(2,128)S(1)}, u32[]{:S(2)}, u32[]{:S(2)}) collective-permute-start(s32[2,768]{1,0:T(2,128)S(1)} %pad_add_fusion), channel_id=1, source_target_pairs={{0,4},{1,5},{2,6},{3,7},{4,0},{5,1},{6,2},{7,3},{8,12},{9,13},{10,... | collective-permute-start | bytes 18440 | tf_op jit(solution)/shard_map/ppermute | solution.py:23
  13.4 15.2 %collective-permute-done.9 = s32[2,768]{1,0:T(2,128)S(1)} collective-permute-done((s32[2,768]{1,0:T(2,128)S(1)}, s32[2,768]{1,0:T(2,128)S(1)}, u32[]{:S(2)}, u32[]{:S(2)}) %collective-permute-start.9) | collective-permute-done | bytes 6176 | tf_op jit(solution)/shard_map/ppermute | solution.py:23
  29.4 1.6 %collective-permute-start.12 = (bf16[256,1024]{1,0:T(8,128)(2,1)S(1)}, bf16[256,1024]{1,0:T(8,128)(2,1)S(1)}, u32[]{:S(2)}, u32[]{:S(2)}) collective-permute-start(bf16[256,1024]{1,0:T(8,128)(2,1)S(1)} %get-tuple-element.18.refs_3_), channel_id=1, source_target_pairs={{0,5},{1,2},{2,7},{3,0},{4,1},{5,6},{6,3},{7,4},{8,13},{9,10},{10,... | collective-permute-start | bytes 1572872 | tf_op jit(solution)/shard_map/ppermute | solution.py:28
  31.2 1.1 %broadcast_select_fusion.2 = (bf16[256,1024]{1,0:T(8,128)(2,1)S(1)}, bf16[256,1024]{1,0:T(8,128)(2,1)S(1)}) fusion(bf16[256,1024]{1,0:T(8,128)(2,1)S(1)} %get-tuple-element.18.refs_3_, pred[]{:T(512)S(6)} %eq.26, bf16[768,1024]{1,0:T(8,128)(2,1)} %source), kind=kLoop, calls=%fused_computation.4 | loop fusion | flops 524288 | bytes 2097153 | tf_op jit(solution)/shard_map/jit(_where)/select_n | solution.py:193
  32.5 0.6 collective-permute-start.1
  33.1 3.1 %shard_map.43.refs_6_ = f32[6,768]{1,0:T(8,128)S(1)} custom-call(bf16[256,1024]{1,0:T(8,128)(2,1)S(1)} %slice.107.refs_0_, bf16[256,1024]{1,0:T(8,128)(2,1)S(1)} %get-tuple-element.19.refs_1_, bf16[256,1024]{1,0:T(8,128)(2,1)S(1)} %get-tuple-element.21.refs_2_, bf16[256,1024]{1,0:T(8,128)(2,1)S(1)} %get-tuple-element.18.refs_3_, ...), custom_call_target="tpu_custom_call" | custom-call | flops 2415919104 | bytes 3145728 | tf_op jit(solution)/shard_map/pallas_call | solution.py:103
  36.3 0.7 %shard_map.44.refs_6_ = f32[6,768]{1,0:T(8,128)S(1)} custom-call(bf16[256,1024]{1,0:T(8,128)(2,1)S(1)} %collective-permute-done.2.refs_0_, bf16[256,1024]{1,0:T(8,128)(2,1)S(1)} %get-tuple-element.28.refs_1_, bf16[256,1024]{1,0:T(8,128)(2,1)S(1)} %get-tuple-element.67.refs_2_, bf16[256,1024]{1,0:T(8,128)(2,1)S(1)} %get-tuple-element.30.refs_3_, ...), custom_call_target="tpu_custom_call" | custom-call | flops 402653184 | bytes 3145728 | tf_op jit(solution)/shard_map/pallas_call | solution.py:139
  37.0 0.8 %shard_map.45.refs_6_ = f32[6,768]{1,0:T(8,128)S(1)} custom-call(bf16[256,1024]{1,0:T(8,128)(2,1)S(1)} %collective-permute-done.4.refs_0_.refs_1_, bf16[256,1024]{1,0:T(8,128)(2,1)S(1)} %get-tuple-element.28.refs_1_, bf16[256,1024]{1,0:T(8,128)(2,1)S(1)} %get-tuple-element.67.refs_2_, bf16[256,1024]{1,0:T(8,128)(2,1)S(1)} %get-tuple-element.30.refs_3_, ...), custom_call_target="tpu_custom_call" | custom-call | flops 402653184 | bytes 3145728 | tf_op jit(solution)/shard_map/pallas_call | solution.py:139
  37.8 0.7 %shard_map.46.refs_8_ = f32[6,768]{1,0:T(8,128)S(1)} custom-call(bf16[256,1024]{1,0:T(8,128)(2,1)S(1)} %collective-permute-done.6.refs_0_.refs_2_, bf16[256,1024]{1,0:T(8,128)(2,1)S(1)} %get-tuple-element.28.refs_1_, bf16[256,1024]{1,0:T(8,128)(2,1)S(1)} %get-tuple-element.67.refs_2_, bf16[256,1024]{1,0:T(8,128)(2,1)S(1)} %get-tuple-element.30.refs_3_, ...), custom_call_target="tpu_custom_call" | custom-call | flops 402653184 | bytes 3145728 | tf_op jit(solution)/shard_map/pallas_call | solution.py:139
  38.5 1.7 %shard_map.47.refs_10_ = f32[6,768]{1,0:T(8,128)S(1)} custom-call(bf16[256,1024]{1,0:T(8,128)(2,1)S(1)} %collective-permute-done.2.refs_0_, bf16[256,1024]{1,0:T(8,128)(2,1)S(1)} %collective-permute-done.4.refs_0_.refs_1_, bf16[256,1024]{1,0:T(8,128)(2,1)S(1)} %collective-permute-done.6.refs_0_.refs_2_, ...), custom_call_target="tpu_custom_call" | custom-call | flops 1207959552 | bytes 3145728 | tf_op jit(solution)/shard_map/pallas_call | solution.py:139
  40.3 1.2 %shard_map.48.refs_10_ = f32[6,768]{1,0:T(8,128)S(1)} custom-call(bf16[256,1024]{1,0:T(8,128)(2,1)S(1)} %collective-permute-done.12.refs_0_, bf16[256,1024]{1,0:T(8,128)(2,1)S(1)} %get-tuple-element.29.refs_1_, bf16[256,1024]{1,0:T(8,128)(2,1)S(1)} %get-tuple-element.66.refs_2_, bf16[256,1024]{1,0:T(8,128)(2,1)S(1)} %get-tuple-element.31.refs_3_, ...), custom_call_target="tpu_custom_call" | custom-call | flops 805306368 | bytes 4718592 | tf_op jit(solution)/shard_map/pallas_call | solution.py:139
  41.5 2.2 %collective-permute-done.11.refs_0_ = bf16[256,1024]{1,0:T(8,128)(2,1)S(1)} collective-permute-done((bf16[256,1024]{1,0:T(8,128)(2,1)S(1)}, bf16[256,1024]{1,0:T(8,128)(2,1)S(1)}, u32[]{:S(2)}, u32[]{:S(2)}) %collective-permute-start.11) | collective-permute-done | bytes 524320 | tf_op jit(solution)/shard_map/ppermute | solution.py:28
  43.7 1.2 %shard_map.49.refs_10_ = f32[6,768]{1,0:T(8,128)S(1)} custom-call(bf16[256,1024]{1,0:T(8,128)(2,1)S(1)} %collective-permute-done.11.refs_0_, bf16[256,1024]{1,0:T(8,128)(2,1)S(1)} %get-tuple-element.29.refs_1_, bf16[256,1024]{1,0:T(8,128)(2,1)S(1)} %get-tuple-element.66.refs_2_, bf16[256,1024]{1,0:T(8,128)(2,1)S(1)} %get-tuple-element.31.refs_3_, ...), custom_call_target="tpu_custom_call" | custom-call | flops 805306368 | bytes 4718592 | tf_op jit(solution)/shard_map/pallas_call | solution.py:139
  44.9 4.4 %collective-permute-done.1.refs_0_ = bf16[256,1024]{1,0:T(8,128)(2,1)S(1)} collective-permute-done((bf16[256,1024]{1,0:T(8,128)(2,1)S(1)}, bf16[256,1024]{1,0:T(8,128)(2,1)S(1)}, u32[]{:S(2)}, u32[]{:S(2)}) %collective-permute-start.1) | collective-permute-done | bytes 524320 | tf_op jit(solution)/shard_map/ppermute | solution.py:28
  49.3 1.2 %shard_map.50 = f32[6,768]{1,0:T(8,128)S(1)} custom-call(bf16[256,1024]{1,0:T(8,128)(2,1)S(1)} %collective-permute-done.1.refs_0_, bf16[256,1024]{1,0:T(8,128)(2,1)S(1)} %get-tuple-element.29.refs_1_, bf16[256,1024]{1,0:T(8,128)(2,1)S(1)} %get-tuple-element.66.refs_2_, bf16[256,1024]{1,0:T(8,128)(2,1)S(1)} %get-tuple-element.31.refs_3_, ...), custom_call_target="tpu_custom_call" | custom-call | flops 805306368 | bytes 4718592 | tf_op jit(solution)/shard_map/pallas_call | solution.py:139
  50.6 1.6 %collective-permute-start.13 = (f32[5,768]{1,0:T(8,128)S(1)}, f32[5,768]{1,0:T(8,128)S(1)}, u32[]{:S(2)}, u32[]{:S(2)}) collective-permute-start(f32[5,768]{1,0:T(8,128)S(1)} %pad_maximum_fusion), channel_id=1, source_target_pairs={{0,5},{1,4},{2,7},{3,6},{4,1},{5,0},{6,3},{7,2},{8,13},{9,12},{10,... | collective-permute-start | bytes 46088 | tf_op jit(solution)/shard_map/ppermute | solution.py:23
  52.2 1.7 %collective-permute-done.13 = f32[5,768]{1,0:T(8,128)S(1)} collective-permute-done((f32[5,768]{1,0:T(8,128)S(1)}, f32[5,768]{1,0:T(8,128)S(1)}, u32[]{:S(2)}, u32[]{:S(2)}) %collective-permute-start.13) | collective-permute-done | bytes 15392 | tf_op jit(solution)/shard_map/ppermute | solution.py:23
  54.0 0.6 collective-permute-start.14
  54.6 2.7 %collective-permute-done.14 = f32[8,768]{1,0:T(8,128)S(1)} collective-permute-done((f32[8,768]{1,0:T(8,128)S(1)}, f32[8,768]{1,0:T(8,128)S(1)}, u32[]{:S(2)}, u32[]{:S(2)}) %collective-permute-start.14) | collective-permute-done | bytes 24608 | tf_op jit(solution)/shard_map/ppermute | solution.py:23
  57.9 1.5 %collective-permute-start.16 = (s32[2,768]{1,0:T(2,128)S(1)}, s32[2,768]{1,0:T(2,128)S(1)}, u32[]{:S(2)}, u32[]{:S(2)}) collective-permute-start(s32[2,768]{1,0:T(2,128)S(1)} %collective-permute-done.10), channel_id=1, source_target_pairs={{0,4},{1,5},{2,6},{3,7},{4,0},{5,1},{6,2},{7,3},{8,12},{9,13},{10,... | collective-permute-start | bytes 18440 | tf_op jit(solution)/shard_map/ppermute | solution.py:23
  59.4 2.1 %collective-permute-done.16 = s32[2,768]{1,0:T(2,128)S(1)} collective-permute-done((s32[2,768]{1,0:T(2,128)S(1)}, s32[2,768]{1,0:T(2,128)S(1)}, u32[]{:S(2)}, u32[]{:S(2)}) %collective-permute-start.16) | collective-permute-done | bytes 6176 | tf_op jit(solution)/shard_map/ppermute | solution.py:23
  62.1 1.2 %collective-permute-start.17 = (f32[128]{0:T(128)S(1)}, f32[128]{0:T(128)S(1)}, u32[]{:S(2)}, u32[]{:S(2)}) collective-permute-start(f32[128]{0:T(128)S(1)} %select_reduce_fusion), channel_id=1, source_target_pairs={{0,9},{1,8},{2,11},{3,10},{4,13},{5,12},{6,15},{7,14},{8,1},{9,0},... | collective-permute-start | bytes 1544 | tf_op jit(solution)/shard_map/ppermute | solution.py:23
  63.3 0.6 slice_reduce_fusion
  63.9 2.2 %collective-permute-done.17 = f32[128]{0:T(128)S(1)} collective-permute-done((f32[128]{0:T(128)S(1)}, f32[128]{0:T(128)S(1)}, u32[]{:S(2)}, u32[]{:S(2)}) %collective-permute-start.17) | collective-permute-done | bytes 544 | tf_op jit(solution)/shard_map/ppermute | solution.py:23
  (44 shorter events, 3.1 us)
Async XLA Ops:
  0.6 12.7 %copy-start.1 = (s32[768]{0:T(1024)S(1)}, s32[768]{0:T(1024)}, u32[]{:S(2)}) copy-start(s32[768]{0:T(1024)} %param.3) | copy-start | bytes 9220
  1.7 27.6 %collective-permute-start = (bf16[768,1024]{1,0:T(8,128)(2,1)}, bf16[768,1024]{1,0:T(8,128)(2,1)S(1)}, u32[]{:S(2)}, u32[]{:S(2)}) collective-permute-start(bf16[768,1024]{1,0:T(8,128)(2,1)} %source), channel_id=1, source_target_pairs={{0,1},{1,0},{2,3},{3,2},{4,5},{5,4},{6,7},{7,6},{8,9},{9,8},{10,11... | collective-permute-start | bytes 4718600 | tf_op jit(solution)/shard_map/ppermute | solution.py:23
  3.0 2.6 %collective-permute-start.8 = (s32[1,768]{1,0:T(1,128)S(1)}, s32[1,768]{1,0:T(1,128)S(1)}, u32[]{:S(2)}, u32[]{:S(2)}) collective-permute-start(s32[1,768]{1,0:T(1,128)S(1)} %broadcast_in_dim.21.refs_6_), channel_id=1, source_target_pairs={{0,1},{1,0},{2,3},{3,2},{4,5},{5,4},{6,7},{7,6},{8,9},{9,8},{10,11... | collective-permute-start | bytes 9224 | tf_op jit(solution)/shard_map/ppermute | solution.py:23
  5.6 6.4 %collective-permute-start.10 = (s32[2,768]{1,0:T(2,128)S(1)}, s32[2,768]{1,0:T(2,128)S(1)}, u32[]{:S(2)}, u32[]{:S(2)}) collective-permute-start(s32[2,768]{1,0:T(2,128)S(1)} %pad_add_fusion), channel_id=1, source_target_pairs={{0,2},{1,3},{2,0},{3,1},{4,6},{5,7},{6,4},{7,5},{8,10},{9,11},{10,... | collective-permute-start | bytes 18440 | tf_op jit(solution)/shard_map/ppermute | solution.py:23
  8.5 20.7 %collective-permute-start.2 = (bf16[256,1024]{1,0:T(8,128)(2,1)S(1)}, bf16[256,1024]{1,0:T(8,128)(2,1)S(1)}, u32[]{:S(2)}, u32[]{:S(2)}) collective-permute-start(bf16[256,1024]{1,0:T(8,128)(2,1)S(1)} %slice.107.refs_0_), channel_id=1, source_target_pairs={{0,5},{1,2},{2,7},{3,0},{4,1},{5,6},{6,3},{7,4},{8,13},{9,10},{10,... | collective-permute-start | bytes 1572872 | tf_op jit(solution)/shard_map/ppermute | solution.py:28
  9.5 1.4 %copy-start = (bf16[768,1024]{1,0:T(8,128)(2,1)S(1)}, bf16[768,1024]{1,0:T(8,128)(2,1)}, u32[]{:S(2)}) copy-start(bf16[768,1024]{1,0:T(8,128)(2,1)} %source) | copy-start | bytes 4718596
  11.0 17.6 %collective-permute-start.4 = (bf16[256,1024]{1,0:T(8,128)(2,1)S(1)}, bf16[256,1024]{1,0:T(8,128)(2,1)S(1)}, u32[]{:S(2)}, u32[]{:S(2)}) collective-permute-start(bf16[256,1024]{1,0:T(8,128)(2,1)S(1)} %get-tuple-element.19.refs_1_), channel_id=1, source_target_pairs={{0,5},{1,2},{2,7},{3,0},{4,1},{5,6},{6,3},{7,4},{8,13},{9,10},{10,... | collective-permute-start | bytes 1572872 | tf_op jit(solution)/shard_map/ppermute | solution.py:28
  11.9 16.8 %collective-permute-start.6 = (bf16[256,1024]{1,0:T(8,128)(2,1)S(1)}, bf16[256,1024]{1,0:T(8,128)(2,1)S(1)}, u32[]{:S(2)}, u32[]{:S(2)}) collective-permute-start(bf16[256,1024]{1,0:T(8,128)(2,1)S(1)} %get-tuple-element.21.refs_2_), channel_id=1, source_target_pairs={{0,5},{1,2},{2,7},{3,0},{4,1},{5,6},{6,3},{7,4},{8,13},{9,10},{10,... | collective-permute-start | bytes 1572872 | tf_op jit(solution)/shard_map/ppermute | solution.py:28
  11.9 16.6 %collective-permute-start.9 = (s32[2,768]{1,0:T(2,128)S(1)}, s32[2,768]{1,0:T(2,128)S(1)}, u32[]{:S(2)}, u32[]{:S(2)}) collective-permute-start(s32[2,768]{1,0:T(2,128)S(1)} %pad_add_fusion), channel_id=1, source_target_pairs={{0,4},{1,5},{2,6},{3,7},{4,0},{5,1},{6,2},{7,3},{8,12},{9,13},{10,... | collective-permute-start | bytes 18440 | tf_op jit(solution)/shard_map/ppermute | solution.py:23
  28.6 3.9 %collective-permute-start.5 = (bf16[256,1024]{1,0:T(8,128)(2,1)S(1)}, bf16[256,1024]{1,0:T(8,128)(2,1)S(1)}, u32[]{:S(2)}, u32[]{:S(2)}) collective-permute-start(bf16[256,1024]{1,0:T(8,128)(2,1)S(1)} %collective-permute-done.4.refs_0_.refs_1_), channel_id=1, source_target_pairs={{0,1},{1,0},{2,3},{3,2},{4,5},{5,4},{6,7},{7,6},{8,9},{9,8},{10,11... | collective-permute-start | bytes 1572872 | tf_op jit(solution)/shard_map/ppermute | solution.py:23
  28.7 9.8 %collective-permute-start.7 = (bf16[256,1024]{1,0:T(8,128)(2,1)S(1)}, bf16[256,1024]{1,0:T(8,128)(2,1)S(1)}, u32[]{:S(2)}, u32[]{:S(2)}) collective-permute-start(bf16[256,1024]{1,0:T(8,128)(2,1)S(1)} %collective-permute-done.6.refs_0_.refs_2_), channel_id=1, source_target_pairs={{0,1},{1,0},{2,3},{3,2},{4,5},{5,4},{6,7},{7,6},{8,9},{9,8},{10,11... | collective-permute-start | bytes 1572872 | tf_op jit(solution)/shard_map/ppermute | solution.py:23
  29.2 9.3 %collective-permute-start.3 = (bf16[256,1024]{1,0:T(8,128)(2,1)S(1)}, bf16[256,1024]{1,0:T(8,128)(2,1)S(1)}, u32[]{:S(2)}, u32[]{:S(2)}) collective-permute-start(bf16[256,1024]{1,0:T(8,128)(2,1)S(1)} %collective-permute-done.2.refs_0_), channel_id=1, source_target_pairs={{0,1},{1,0},{2,3},{3,2},{4,5},{5,4},{6,7},{7,6},{8,9},{9,8},{10,11... | collective-permute-start | bytes 1572872 | tf_op jit(solution)/shard_map/ppermute | solution.py:23
  29.4 10.8 %collective-permute-start.12 = (bf16[256,1024]{1,0:T(8,128)(2,1)S(1)}, bf16[256,1024]{1,0:T(8,128)(2,1)S(1)}, u32[]{:S(2)}, u32[]{:S(2)}) collective-permute-start(bf16[256,1024]{1,0:T(8,128)(2,1)S(1)} %get-tuple-element.18.refs_3_), channel_id=1, source_target_pairs={{0,5},{1,2},{2,7},{3,0},{4,1},{5,6},{6,3},{7,4},{8,13},{9,10},{10,... | collective-permute-start | bytes 1572872 | tf_op jit(solution)/shard_map/ppermute | solution.py:28
  31.0 12.7 %collective-permute-start.11 = (bf16[256,1024]{1,0:T(8,128)(2,1)S(1)}, bf16[256,1024]{1,0:T(8,128)(2,1)S(1)}, u32[]{:S(2)}, u32[]{:S(2)}) collective-permute-start(bf16[256,1024]{1,0:T(8,128)(2,1)S(1)} %get-tuple-element.20.refs_4_), channel_id=1, source_target_pairs={{0,5},{1,2},{2,7},{3,0},{4,1},{5,6},{6,3},{7,4},{8,13},{9,10},{10,... | collective-permute-start | bytes 1572872 | tf_op jit(solution)/shard_map/ppermute | solution.py:28
  32.5 16.8 %collective-permute-start.1 = (bf16[256,1024]{1,0:T(8,128)(2,1)S(1)}, bf16[256,1024]{1,0:T(8,128)(2,1)S(1)}, u32[]{:S(2)}, u32[]{:S(2)}) collective-permute-start(bf16[256,1024]{1,0:T(8,128)(2,1)S(1)} %get-tuple-element.16.refs_5_), channel_id=1, source_target_pairs={{0,5},{1,2},{2,7},{3,0},{4,1},{5,6},{6,3},{7,4},{8,13},{9,10},{10,... | collective-permute-start | bytes 1572872 | tf_op jit(solution)/shard_map/ppermute | solution.py:28
  50.6 3.3 %collective-permute-start.13 = (f32[5,768]{1,0:T(8,128)S(1)}, f32[5,768]{1,0:T(8,128)S(1)}, u32[]{:S(2)}, u32[]{:S(2)}) collective-permute-start(f32[5,768]{1,0:T(8,128)S(1)} %pad_maximum_fusion), channel_id=1, source_target_pairs={{0,5},{1,4},{2,7},{3,6},{4,1},{5,0},{6,3},{7,2},{8,13},{9,12},{10,... | collective-permute-start | bytes 46088 | tf_op jit(solution)/shard_map/ppermute | solution.py:23
  54.0 3.3 %collective-permute-start.14 = (f32[8,768]{1,0:T(8,128)S(1)}, f32[8,768]{1,0:T(8,128)S(1)}, u32[]{:S(2)}, u32[]{:S(2)}) collective-permute-start(f32[8,768]{1,0:T(8,128)S(1)} %add.28), channel_id=1, source_target_pairs={{0,3},{1,2},{2,1},{3,0},{4,7},{5,6},{6,5},{7,4},{8,11},{9,10},{10,... | collective-permute-start | bytes 73736 | tf_op jit(solution)/shard_map/ppermute | solution.py:23
  57.4 4.2 %collective-permute-start.15 = (f32[8,768]{1,0:T(8,128)S(1)}, f32[8,768]{1,0:T(8,128)S(1)}, u32[]{:S(2)}, u32[]{:S(2)}) collective-permute-start(f32[8,768]{1,0:T(8,128)S(1)} %add.29), channel_id=1, source_target_pairs={{0,1},{1,0},{2,3},{3,2},{4,5},{5,4},{6,7},{7,6},{8,9},{9,8},{10,11... | collective-permute-start | bytes 73736 | tf_op jit(solution)/shard_map/ppermute | solution.py:23
  57.9 3.6 %collective-permute-start.16 = (s32[2,768]{1,0:T(2,128)S(1)}, s32[2,768]{1,0:T(2,128)S(1)}, u32[]{:S(2)}, u32[]{:S(2)}) collective-permute-start(s32[2,768]{1,0:T(2,128)S(1)} %collective-permute-done.10), channel_id=1, source_target_pairs={{0,4},{1,5},{2,6},{3,7},{4,0},{5,1},{6,2},{7,3},{8,12},{9,13},{10,... | collective-permute-start | bytes 18440 | tf_op jit(solution)/shard_map/ppermute | solution.py:23
  62.1 4.0 %collective-permute-start.17 = (f32[128]{0:T(128)S(1)}, f32[128]{0:T(128)S(1)}, u32[]{:S(2)}, u32[]{:S(2)}) collective-permute-start(f32[128]{0:T(128)S(1)} %select_reduce_fusion), channel_id=1, source_target_pairs={{0,9},{1,8},{2,11},{3,10},{4,13},{5,12},{6,15},{7,14},{8,1},{9,0},... | collective-permute-start | bytes 1544 | tf_op jit(solution)/shard_map/ppermute | solution.py:23
